TPU v7x, 256 devices: a whole 4x4x8 slice. The times are simulated.
256 devices in a mesh: node: 16 (over x, z_hi), tm: 16 (over z_lo, y, core).
Axes of the slice: x: 4, y: 4, z: 8 (z_hi: 4, z_lo: 2; z = z_hi * 2 + z_lo), core: 2. Of those that a mesh axis runs over, the one named last changes fastest.
Arguments:
- codes: int32 [65536, 2048], P('node', 'tm'), may hold values from -127 to 127
- node_scale: float32 [65536], P('node'), may hold values from 0.002 to 0.02
- basis: bfloat16 [65536, 128], P('node'), may hold values from -0.0234375 to 0.0234375
- regular: float32 [8384], replicated, may hold values from 0.05 to 0.5
- feature_order: int32 [8384], replicated, may hold values from 0 to 8383, each once
- panel_inverse: float32 [2, 262, 262], replicated, may hold values from -0.06 to 1.2
Outputs:
- schur: float32 [8384, 8384], P('node', 'tm')
Inputs may be any that keep to these rules, and one draw needn't show every extreme that they name: `feature_order`: a permutation: every feature stands at exactly one position.
All inputs are finite; a program needn't handle non-finite values.
Results may differ from a plain program's by a relative error of at most 0.0051.
Values sent between devices are 32-bit elements; how exact they have to be, the bound alone decides.
A program may use at most 64 MiB of HBM per device.

v0:
```python
import jax
import jax.numpy as jnp
import numpy as np
from jax import lax
from jax.sharding import PartitionSpec as P


def from_root(block, axis, source):
    block = jnp.where(lax.axis_index(axis) == source, block, jnp.zeros_like(block))
    return lax.psum(block, axis)


def pair_tables(rank_count):
    former_list = []
    latter_list = []
    for leading in range(rank_count + 1):
        for trailing in range(leading, rank_count + 1):
            if leading < rank_count or trailing < rank_count:
                former_list.append(leading)
                latter_list.append(trailing)
    return (np.array(former_list, np.int32), np.array(latter_list, np.int32))


def selectors(chosen, rank_count):
    former, latter = pair_tables(rank_count)
    leading = jnp.take(jnp.asarray(former), chosen)
    trailing = jnp.take(jnp.asarray(latter), chosen)
    lead_index = jnp.minimum(leading, rank_count - 1)
    trail_index = jnp.minimum(trailing, rank_count - 1)
    lead_keep = (leading < rank_count).astype(jnp.float32)
    trail_keep = (trailing < rank_count).astype(jnp.float32)
    return (lead_index, lead_keep, trail_index, trail_keep)


def make_features(window, picks):
    lead_index, lead_keep, trail_index, trail_keep = picks
    lead_vals = (
        jnp.take(window, lead_index, axis=1) * lead_keep[None, :] + (1.0 - lead_keep)[None, :]
    )
    trail_vals = (
        jnp.take(window, trail_index, axis=1) * trail_keep[None, :] + (1.0 - trail_keep)[None, :]
    )
    return (lead_vals * trail_vals).astype(jnp.bfloat16)


def contract(left_feats, right_feats):
    return lax.dot_general(
        left_feats, right_feats, (((0,), (0,)), ((), ())), preferred_element_type=jnp.float32
    )


def highest(left_mat, right_mat):
    return jnp.dot(
        left_mat, right_mat, precision=lax.Precision.HIGHEST, preferred_element_type=jnp.float32
    )


def per_device(codes, node_scale, basis, regular, feature_order, panel_inverse):
    rank_count = basis.shape[1]
    snap_local = codes.shape[1]
    nfeat = regular.shape[0]
    row_size = nfeat // lax.axis_size("node")
    col_size = nfeat // lax.axis_size("tm")
    snap_total = snap_local * lax.axis_size("tm")
    panel_count = panel_inverse.shape[0]
    panel_width = panel_inverse.shape[1]
    scaled_basis = (basis.astype(jnp.float32) * node_scale[:, None]).astype(jnp.bfloat16)
    code_values = codes.astype(jnp.bfloat16)
    row_offset = lax.axis_index("node") * row_size
    col_offset = lax.axis_index("tm") * col_size
    row_picks = selectors(lax.dynamic_slice_in_dim(feature_order, row_offset, row_size), rank_count)
    col_picks = selectors(lax.dynamic_slice_in_dim(feature_order, col_offset, col_size), rank_count)
    empty_tile = jnp.zeros((row_size, col_size), jnp.float32)
    window = code_values
    summed = lax.psum(
        lax.dot_general(
            window, scaled_basis, (((0,), (0,)), ((), ())), preferred_element_type=jnp.float32
        ),
        "node",
    )
    running = empty_tile
    portion = lax.all_gather(summed, "tm", axis=0, tiled=True)
    length = portion.shape[0]
    stride = min(length, 1024)
    for anchor in range(0, length, stride):
        window = portion[anchor : anchor + stride]
        running = running + contract(
            make_features(window, row_picks), make_features(window, col_picks)
        )
    row_global = row_offset + jnp.arange(row_size, dtype=jnp.int32)
    col_global = col_offset + jnp.arange(col_size, dtype=jnp.int32)
    on_diagonal = (row_global[:, None] == col_global[None, :]).astype(jnp.float32)
    row_regular = lax.dynamic_slice_in_dim(regular, row_offset, row_size)
    matrix = running / snap_total + on_diagonal * row_regular[:, None]
    for panel_number in range(panel_count):
        local_panel_lower = panel_number * panel_width
        col_start = local_panel_lower - local_panel_lower // col_size * col_size
        row_start = local_panel_lower - local_panel_lower // row_size * row_size
        col_start, row_start = (col_start, row_start)
        panel_lower = panel_number * panel_width
        left_part = from_root(
            matrix[:, col_start : col_start + panel_width], "tm", panel_lower // col_size
        )
        upper_part = from_root(
            matrix[row_start : row_start + panel_width, :], "node", panel_lower // row_size
        )
        left_part, upper_part = (left_part, upper_part)
        scaled_left = highest(left_part, panel_inverse[panel_number])
        matrix = matrix - highest(scaled_left, upper_part)
    return matrix


def solution(mesh):
    placed = (P("node", "tm"), P("node"), P("node", None), P(), P(), P())
    return jax.shard_map(
        per_device, mesh=mesh, in_specs=placed, out_specs=P("node", "tm"), check_vma=False
    )
```

profile of v0, /device:TPU:1, one launch (start us, length us, event | category | flops | bytes accessed | tf_op | source)
XLA Modules:
  0.0 823.1 jit_solution(677278709692497030)
XLA Ops:
  6.5 3.7 convolution_bitcast_fusion
  11.1 147.0 %all-reduce.6.cloned.1.call-done = f32[128,128]{0,1:T(8,128)} async-done(((f32[128,128]{0,1:T(8,128)}), f32[128,128]{0,1:T(8,128)}) %all-reduce.6.cloned.1.call-update) | async-done | bytes 65552 | tf_op jit(solution)/shard_map/psum | solution.py:75
  158.2 3.6 gather_fusion.4
  161.8 3.6 gather_fusion.6
  165.3 3.6 gather_fusion
  168.9 3.6 gather_fusion.2
  173.4 29.3 %all-gather.2.cloned.1.call-done = f32[2048,128]{0,1:T(8,128)} async-done(((f32[128,128]{0,1:T(8,128)}), f32[2048,128]{0,1:T(8,128)}) %all-gather.2.cloned.1.call-update) | async-done | bytes 1048592 | tf_op jit(solution)/shard_map/all_gather | solution.py:82
  204.0 2.5 gather_fusion.7
  206.4 3.3 gather_fusion.3
  209.7 3.3 gather_fusion.9
  213.0 3.3 gather_fusion.11
  216.3 3.3 gather_fusion.1
  219.5 3.3 gather_fusion.8
  222.8 3.3 gather_fusion.5
  226.0 3.3 gather_fusion.10
  229.4 4.9 fusion.18
  240.3 117.6 %all-reduce.8.cloned.1.call-done = f32[524,262]{1,0:T(8,128)} async-done(((f32[524,262]{1,0:T(8,128)}), f32[524,262]{1,0:T(8,128)}) %all-reduce.8.cloned.1.call-update) | async-done | bytes 549168 | tf_op jit(solution)/shard_map/psum | solution.py:10
  358.0 2.8 fusion.52
  360.8 158.2 %all-reduce.10.cloned.1.call-done = f32[262,524]{1,0:T(8,128)} async-done(((f32[262,524]{1,0:T(8,128)}), f32[262,524]{1,0:T(8,128)}) %all-reduce.10.cloned.1.call-update) | async-done | bytes 549168 | tf_op jit(solution)/shard_map/psum | solution.py:10
  518.9 3.7 convolution_subtract_fusion.1
  524.8 125.8 %all-reduce.12.cloned.1.call-done = f32[524,262]{1,0:T(8,128)} async-done(((f32[524,262]{1,0:T(8,128)}), f32[524,262]{1,0:T(8,128)}) %all-reduce.12.cloned.1.call-update) | async-done | bytes 549168 | tf_op jit(solution)/shard_map/psum | solution.py:10
  650.6 2.8 fusion.51
  653.5 158.1 %all-reduce.14.cloned.1.call-done = f32[262,524]{1,0:T(8,128)} async-done(((f32[262,524]{1,0:T(8,128)}), f32[262,524]{1,0:T(8,128)}) %all-reduce.14.cloned.1.call-update) | async-done | bytes 549168 | tf_op jit(solution)/shard_map/psum | solution.py:10
  811.6 4.7 convolution_subtract_fusion
  (49 shorter events, 11.3 us)
Async XLA Ops:
  6.5 151.7 %copy-start.1 = (s32[8384]{0:T(1024)S(1)}, s32[8384]{0:T(1024)}, u32[]{:S(2)}) copy-start(s32[8384]{0:T(1024)} %constant.50.clone2.2) | copy-start | bytes 100612
  6.5 151.6 %all-reduce.6.cloned.1.call-start = ((), (), s32[]{:S(2)}) async-start(), calls=%async_computation | async-start | bytes 131072 | tf_op jit(solution)/shard_map/psum | solution.py:75
  10.2 192.5 %all-gather.2.cloned.1.call-start = ((), (), s32[]{:S(2)}) async-start(), calls=%async_computation.1 | async-start | bytes 1114112 | tf_op jit(solution)/shard_map/all_gather | solution.py:82
  10.3 151.5 %copy-start = (s32[8384]{0:T(1024)S(1)}, s32[8384]{0:T(1024)}, u32[]{:S(2)}) copy-start(s32[8384]{0:T(1024)} %constant.51.clone2.2) | copy-start | bytes 100612
  158.1 199.8 %all-reduce.8.cloned.1.call-start = ((), (), s32[]{:S(2)}) async-start(), calls=%async_computation.2 | async-start | bytes 1622016 | tf_op jit(solution)/shard_map/psum | solution.py:10
  229.3 4.9 copy-start.2
  229.3 4.9 copy-start.3
  229.3 4.9 copy-start.4
  229.3 5.5 copy-start.5
  236.7 2.2 copy-start.7
  237.7 281.2 %all-reduce.10.cloned.1.call-start = ((), (), s32[]{:S(2)}) async-start(), calls=%async_computation.3 | async-start | bytes 1351680 | tf_op jit(solution)/shard_map/psum | solution.py:10
  238.7 411.9 %all-reduce.12.cloned.1.call-start = ((), (), s32[]{:S(2)}) async-start(), calls=%async_computation.4 | async-start | bytes 1622016 | tf_op jit(solution)/shard_map/psum | solution.py:10
  522.6 128.0 %copy-start.6 = (f32[1,262,262]{2,0,1:T(1,128)S(1)}, f32[1,262,262]{2,0,1:T(1,128)}, u32[]{:S(2)}) copy-start(f32[1,262,262]{2,0,1:T(1,128)} %get-tuple-element.27) | copy-start | bytes 823732
  523.8 287.8 %all-reduce.14.cloned.1.call-start = ((), (), s32[]{:S(2)}) async-start(), calls=%async_computation.5 | async-start | bytes 1351680 | tf_op jit(solution)/shard_map/psum | solution.py:10
Sparse Core Ops, SparseCore 0:
  10.3 147.7 all-reduce.5
  160.0 42.6 all-gather.1
  237.8 120.0 all-reduce.7
  360.4 158.4 all-reduce.9
  523.9 126.6 all-reduce.11
  653.1 158.4 all-reduce.13
where the time goes:
time: 833 us; the launch traced here: 823 us
  waiting for transfers between devices  736 us (88%)
  local copies, waits for them, and re-layouts  43.5 us (5%)
  matrix products  24.5 us (3%)
  between operations  13.7 us (2%)
    psum x4, waiting for transfers between devices, from_root(): return lax.psum(block, axis)  560 us
    psum x1, waiting for transfers between devices, per_device(): lax.psum(lax.dot_general(window, scaled_basis, (((0,), (0,)), ((), ())),...  147 us
    all_gather x1, waiting for transfers between devices, per_device(): portion = lax.all_gather(summed, 'tm', axis=0, tiled=True)  29.3 us
  transfers between devices with their start and end apart: 6, of which 6 were waited for; matrix products, arithmetic and copies ran while one was open for 3% of the time, Pallas kernels for 0%

commit v1 on v0

v1 whole, which is shorter than its diff:
```python
import jax
import jax.numpy as jnp
import numpy as np
from jax import lax
from jax.sharding import PartitionSpec as P


def pair_starts(rank_count):
    leading = np.arange(rank_count + 1)
    return (leading * (rank_count + 1) - leading * (leading - 1) // 2).astype(np.int32)


def selectors(chosen, rank_count):
    starts = pair_starts(rank_count)
    modes = jnp.arange(rank_count, dtype=jnp.int32)
    below = chosen[:, None] >= jnp.asarray(starts[:-1])[None, :]
    above = chosen[:, None] < jnp.asarray(starts[1:])[None, :]
    lead = jnp.logical_and(below, above)
    shift = modes - jnp.asarray(starts[:-1])
    trailing = chosen + jnp.sum(jnp.where(lead, shift[None, :], 0), axis=1)
    trail = trailing[:, None] == modes[None, :]
    keep = (trailing < rank_count).astype(jnp.float32)
    return lead.astype(jnp.bfloat16), trail.astype(jnp.bfloat16), 1.0 - keep


def spread(values):
    high = lax.reduce_precision(values, 8, 7)
    low = lax.reduce_precision(values - high, 8, 7)
    return jnp.concatenate([high, low], axis=1).astype(jnp.bfloat16)


def make_features(pieces, picks):
    lead, trail, constant = picks
    dims = (((1,), (1,)), ((), ()))
    lead = jnp.concatenate([lead, lead], axis=1)
    trail = jnp.concatenate([trail, trail], axis=1)
    lead_vals = lax.dot_general(lead, pieces, dims, preferred_element_type=jnp.float32)
    trail_vals = lax.dot_general(trail, pieces, dims, preferred_element_type=jnp.float32)
    return (lead_vals * (trail_vals + constant[:, None])).astype(jnp.bfloat16)


def contract(left_feats, right_feats):
    return lax.dot_general(
        left_feats, right_feats, (((1,), (1,)), ((), ())), preferred_element_type=jnp.float32
    )


def highest(left_mat, right_mat):
    return jnp.dot(
        left_mat, right_mat, precision=lax.Precision.HIGHEST, preferred_element_type=jnp.float32
    )


def per_device(codes, node_scale, basis, regular, feature_order, panel_inverse):
    rank_count = basis.shape[1]
    snap_local = codes.shape[1]
    nfeat = regular.shape[0]
    row_size = nfeat // lax.axis_size("node")
    col_size = nfeat // lax.axis_size("tm")
    snap_total = snap_local * lax.axis_size("tm")
    panel_width = panel_inverse.shape[1]
    span = 2 * panel_width
    scaled_basis = (basis.astype(jnp.float32) * node_scale[:, None]).astype(jnp.bfloat16)
    code_values = codes.astype(jnp.bfloat16)
    row_offset = lax.axis_index("node") * row_size
    col_offset = lax.axis_index("tm") * col_size
    row_picks = selectors(lax.dynamic_slice_in_dim(feature_order, row_offset, row_size), rank_count)
    col_picks = selectors(lax.dynamic_slice_in_dim(feature_order, col_offset, col_size), rank_count)
    pan_picks = selectors(feature_order[:span], rank_count)
    summed = lax.psum(
        lax.dot_general(
            code_values, scaled_basis, (((0,), (0,)), ((), ())), preferred_element_type=jnp.float32
        ),
        "node",
    )
    pieces = spread(lax.all_gather(summed, "tm", axis=0, tiled=True))
    row_feats = make_features(pieces, row_picks)
    col_feats = make_features(pieces, col_picks)
    pan_feats = make_features(pieces, pan_picks)
    row_global = row_offset + jnp.arange(row_size, dtype=jnp.int32)
    col_global = col_offset + jnp.arange(col_size, dtype=jnp.int32)
    pan_global = jnp.arange(span, dtype=jnp.int32)
    row_regular = lax.dynamic_slice_in_dim(regular, row_offset, row_size)

    def block(left_feats, right_feats, left_global, right_global, left_regular):
        same = (left_global[:, None] == right_global[None, :]).astype(jnp.float32)
        return contract(left_feats, right_feats) / snap_total + same * left_regular[:, None]

    matrix = block(row_feats, col_feats, row_global, col_global, row_regular)
    left = block(row_feats, pan_feats, row_global, pan_global, row_regular)
    upper = block(pan_feats, col_feats, pan_global, col_global, regular[:span])
    w = panel_width
    inner = contract(pan_feats[:w], pan_feats[w:]) / snap_total
    first_left = highest(left[:, :w], panel_inverse[0])
    second_left = left[:, w:] - highest(first_left, inner)
    cross = highest(panel_inverse[0], inner)
    second_upper = upper[w:] - highest(cross.T, upper[:w])
    second_left = highest(second_left, panel_inverse[1])
    joint = jnp.concatenate([first_left, second_left], axis=1)
    return matrix - highest(joint, jnp.concatenate([upper[:w], second_upper], axis=0))


def solution(mesh):
    placed = (P("node", "tm"), P("node"), P("node", None), P(), P(), P())
    return jax.shard_map(
        per_device, mesh=mesh, in_specs=placed, out_specs=P("node", "tm"), check_vma=False
    )
```

time: 833 us -> 237 us (0.28); the launches traced: 823 us -> 236 us
  waiting for transfers between devices: 736 us -> 188 us
  local copies, waits for them, and re-layouts: 43.5 us -> 2.42 us
    psum x5 -> x1, waiting for transfers between devices: 707 us -> 147 us  [per_device(): lax.psum(lax.dot_general(code_values, scaled_basis, (((0,), (0,)), ((), (...]
    gather x12 -> x0, local copies, waits for them, and re-layouts: 39.6 us -> none  [the longest x4 13.1 us: make_features(): jnp.take(window, lead_index, axis=1) * lead_keep[None, :]]
    all_gather x1, waiting for transfers between devices: 29.3 us -> 41.1 us  [per_device(): pieces = spread(lax.all_gather(summed, 'tm', axis=0, tiled=True))]
  transfers between devices with their start and end apart: 6 -> 2, of which waited for: 6 -> 2; matrix products, arithmetic and copies ran while one was open for 3% -> 2% of each run, Pallas kernels for 0% -> 0%
where the time goes in v1:
time: 237 us; the launch traced here: 236 us
  waiting for transfers between devices  188 us (79%)
  matrix products  28.9 us (12%)
  between operations  13.6 us (6%)
  other arithmetic  3.34 us (1%)
  local copies, waits for them, and re-layouts  2.42 us (1%)
    psum x1, waiting for transfers between devices, per_device(): lax.psum(lax.dot_general(code_values, scaled_basis, (((0,), (0,)), ((), (...  147 us
    all_gather x1, waiting for transfers between devices, per_device(): pieces = spread(lax.all_gather(summed, 'tm', axis=0, tiled=True))  41.1 us
    dot_general x6, matrix products, highest(): jnp.dot(left_mat, right_mat, precision=lax.Precision.HIGHEST, preferred_e...  14 us
    dot_general x4, matrix products, contract(): lax.dot_general(left_feats, right_feats, (((1,), (1,)), ((), ())), prefer...  6.5 us
  transfers between devices with their start and end apart: 2, of which 2 were waited for; matrix products, arithmetic and copies ran while one was open for 2% of the time, Pallas kernels for 0%

profile of v1, /device:TPU:1, one launch (start us, length us, event | category | flops | bytes accessed | tf_op | source)
XLA Modules:
  0.0 236.5 jit_solution(14011582777847682140)
XLA Ops:
  6.6 3.7 %convolution_bitcast_fusion = f32[128,128]{0,1:T(8,128)} fusion(bf16[4096,128]{1,0:T(8,128)(2,1)} %param.17, s32[4096,128]{1,0:T(8,128)} %param.15, f32[4096]{0:T(1024)} %param.16), kind=kOutput, calls=%fused_computation.24 | convolution fusion | flops 136314880 | bytes 3227648 | tf_op jit(solution)/shard_map/dot_general | solution.py:71
  10.4 0.9 fusion.50
  11.3 147.1 %all-reduce.2.cloned.1.call-done = f32[128,128]{0,1:T(8,128)} async-done(((f32[128,128]{0,1:T(8,128)}), f32[128,128]{0,1:T(8,128)}) %all-reduce.2.cloned.1.call-update) | async-done | bytes 65552 | tf_op jit(solution)/shard_map/psum | solution.py:70
  159.0 0.9 fusion.49
  159.8 0.7 convert_subtract_fusion
  161.2 0.6 fusion.48
  161.9 41.1 %all-gather.2.cloned.1.call-done = f32[2048,128]{0,1:T(8,128)} async-done(((f32[128,128]{0,1:T(8,128)}), f32[2048,128]{0,1:T(8,128)}) %all-gather.2.cloned.1.call-update) | async-done | bytes 1048592 | tf_op jit(solution)/shard_map/all_gather | solution.py:76
  202.9 1.4 reduce-precision_convert_fusion
  204.3 0.7 fusion.17
  205.1 0.7 fusion.24
  205.8 0.7 fusion.31
  206.5 0.9 multiply_convert_fusion
  207.4 0.8 convolution_multiply_fusion.3
  208.2 0.8 multiply_convert_fusion.2
  209.0 2.0 fusion.1
  211.0 1.6 fusion.15
  212.6 1.9 fusion.39
  214.5 2.2 convolution_subtract_fusion.1
  216.7 0.8 multiply_convert_fusion.1
  217.5 1.9 fusion
  219.4 1.9 fusion.2
  221.3 1.5 convolution_subtract_fusion.2
  222.8 1.6 fusion.38
  224.4 5.2 %convolution_subtract_fusion = f32[524,524]{1,0:T(8,128)} fusion(f32[524,524]{1,0:T(8,128)S(1)} %fusion, f32[524,262]{0,1:T(8,128)S(1)} %fusion.38, f32[524,262]{0,1:T(8,128)S(1)} %fusion.15, f32[262,524]{1,0:T(8,128)S(1)} %convolution_subtract_fusion.2, f32[262,524]{1,0:T(8,128)S(1)} %slice.46), kind=kOutput, calls=%fused_computation.6 | convolution fusion | flops 1727357696 | bytes 4393216 | tf_op jit(solution)/shard_map/dot_general | solution.py:49
  (20 shorter events, 1.4 us)
Async XLA Ops:
  6.5 151.8 %copy-start.1 = (s32[128]{0:T(128)S(1)}, s32[128]{0:T(128)}, u32[]{:S(2)}) copy-start(s32[128]{0:T(128)} %constant.33.clone) | copy-start | bytes 1540
  6.5 151.8 %copy-start.2 = (s32[128]{0:T(128)S(1)}, s32[128]{0:T(128)}, u32[]{:S(2)}) copy-start(s32[128]{0:T(128)} %constant.32.clone) | copy-start | bytes 1540
  6.5 151.8 %copy-start.3 = (s32[128]{0:T(128)S(1)}, s32[128]{0:T(128)}, u32[]{:S(2)}) copy-start(s32[128]{0:T(128)} %constant.35) | copy-start | bytes 1540
  6.5 154.7 %copy-start = (f32[2,262,262]{2,0,1:T(2,128)S(1)}, f32[2,262,262]{2,0,1:T(2,128)}, u32[]{:S(2)}) copy-start(f32[2,262,262]{2,0,1:T(2,128)} %param.20) | copy-start | bytes 1647460
  6.5 151.8 %all-reduce.2.cloned.1.call-start = ((), (), s32[]{:S(2)}) async-start(), calls=%async_computation | async-start | bytes 131072 | tf_op jit(solution)/shard_map/psum | solution.py:70
  10.3 192.6 %all-gather.2.cloned.1.call-start = ((), (), s32[]{:S(2)}) async-start(), calls=%async_computation.1 | async-start | bytes 1114112 | tf_op jit(solution)/shard_map/all_gather | solution.py:76
Sparse Core Ops, SparseCore 0:
  10.4 147.8 all-reduce.1
  160.2 42.6 all-gather.1

commit v2 on v1

--- a/solution.py
+++ b/solution.py
@@ -2,7 +2,11 @@
 import jax.numpy as jnp
 import numpy as np
 from jax import lax
+from jax.experimental import pallas as pl
+from jax.experimental.pallas import tpu as pltpu
 from jax.sharding import PartitionSpec as P
+
+MESH = pl.DeviceIdType.MESH
 
 
 def pair_starts(rank_count):
@@ -51,6 +55,185 @@
     )
 
 
+def gather_kernel(
+    scale_ref, codes_hbm, basis_hbm, out_ref,
+    codes_buf, basis_buf, total, partial, slots,
+    code_sem, basis_sem, rs_send, rs_recv, z_send, z_recv, xy_send, xy_recv, sib_send, sib_recv,
+):
+    node, tm = lax.axis_index("node"), lax.axis_index("tm")
+    x, z_hi = lax.div(node, 4), lax.rem(node, 4)
+    z_lo, y, core = lax.div(tm, 8), lax.rem(lax.div(tm, 2), 4), lax.rem(tm, 2)
+    z = z_hi * 2 + z_lo
+
+    def place(at_x, at_y, at_z, at_core):
+        return (at_x * 4 + lax.div(at_z, 2), lax.rem(at_z, 2) * 8 + at_y * 2 + at_core)
+
+    def node_peer(step):
+        return (lax.rem(node + step, 16), tm)
+
+    def z_peer(step):
+        return place(x, y, lax.rem(z + step, 8), core)
+
+    def xy_peer(step):
+        return place(lax.rem(x + lax.div(step, 4), 4), lax.rem(y + lax.rem(step, 4), 4), z, core)
+
+    sibling = place(x, y, z, 1 - core)
+
+    chunks = code_sem.shape[0]
+    rows = codes_buf.shape[0] // chunks
+    for chunk in range(chunks):
+        part = pl.ds(chunk * rows, rows)
+        pltpu.make_async_copy(codes_hbm.at[part], codes_buf.at[part], code_sem.at[chunk]).start()
+        pltpu.make_async_copy(basis_hbm.at[part], basis_buf.at[part], basis_sem.at[chunk]).start()
+
+    barrier = pltpu.get_barrier_semaphore()
+
+    def greet(peer):
+        pl.semaphore_signal(barrier, inc=1, device_id=peer, device_id_type=MESH)
+
+    @pl.loop(1, 16)
+    def _(step):
+        greet(node_peer(step))
+        greet(xy_peer(step))
+
+    @pl.loop(1, 8)
+    def _(step):
+        greet(z_peer(step))
+
+    greet(sibling)
+
+    total[...] = jnp.zeros_like(total)
+    for chunk in range(chunks):
+        part = pl.ds(chunk * rows, rows)
+        pltpu.make_async_copy(codes_hbm.at[part], codes_buf.at[part], code_sem.at[chunk]).wait()
+        pltpu.make_async_copy(basis_hbm.at[part], basis_buf.at[part], basis_sem.at[chunk]).wait()
+        turned = []
+        for piece in range(rows // 128):
+            row = chunk * (rows // 128) + piece
+            basis = basis_buf[pl.ds(row * 128, 128), :].astype(jnp.float32)
+            turned.append((basis.T * scale_ref[row : row + 1, :]).astype(jnp.bfloat16))
+        turned = jnp.concatenate(turned, axis=1)
+        values = codes_buf[part, :].astype(jnp.float32).astype(jnp.bfloat16)
+        total[...] += jnp.dot(turned, values, preferred_element_type=jnp.float32)
+    partial[...] = total[...].T.reshape(partial.shape)
+
+    pl.semaphore_wait(barrier, 38)
+
+    def rs_copy(step):
+        peer = node_peer(step)
+        return pltpu.make_async_remote_copy(
+            src_ref=partial.at[peer[0]], dst_ref=slots.at[step],
+            send_sem=rs_send.at[step], recv_sem=rs_recv.at[step],
+            device_id=peer, device_id_type=MESH,
+        )
+
+    block = (x * 4 + y) * 2 + core
+
+    def z_copy(step):
+        return pltpu.make_async_remote_copy(
+            src_ref=out_ref.at[block * 8 + z], dst_ref=out_ref.at[block * 8 + z],
+            send_sem=z_send.at[step], recv_sem=z_recv.at[step],
+            device_id=z_peer(step), device_id_type=MESH,
+        )
+
+    def xy_copy(step):
+        part = pl.ds(block * 8, 8)
+        return pltpu.make_async_remote_copy(
+            src_ref=out_ref.at[part], dst_ref=out_ref.at[part],
+            send_sem=xy_send.at[step], recv_sem=xy_recv.at[step],
+            device_id=xy_peer(step), device_id_type=MESH,
+        )
+
+    def sib_copy(step):
+        from_x = lax.rem(x + 4 - lax.div(step, 4), 4)
+        from_y = lax.rem(y + 4 - lax.rem(step, 4), 4)
+        part = pl.ds(((from_x * 4 + from_y) * 2 + core) * 8, 8)
+        return pltpu.make_async_remote_copy(
+            src_ref=out_ref.at[part], dst_ref=out_ref.at[part],
+            send_sem=sib_send.at[step], recv_sem=sib_recv.at[step],
+            device_id=sibling, device_id_type=MESH,
+        )
+
+    @pl.loop(1, 16)
+    def _(step):
+        rs_copy(step).start()
+
+    @pl.loop(1, 16)
+    def _(step):
+        rs_copy(step).wait_recv()
+
+    summed = partial[node]
+    for step in range(1, 16):
+        summed = summed + slots[step]
+    out_ref[block * 8 + z] = summed
+
+    @pl.loop(1, 8)
+    def _(step):
+        z_copy(step).start()
+
+    @pl.loop(1, 8)
+    def _(step):
+        z_copy(step).wait_recv()
+
+    @pl.loop(1, 16)
+    def _(step):
+        xy_copy(step).start()
+
+    sib_copy(0).start()
+
+    @pl.loop(1, 16)
+    def _(step):
+        xy_copy(step).wait_recv()
+        sib_copy(step).start()
+
+    @pl.loop(0, 16)
+    def _(step):
+        sib_copy(step).wait_recv()
+
+    sib_copy(0).wait_send()
+
+    @pl.loop(1, 16)
+    def _(step):
+        rs_copy(step).wait_send()
+        xy_copy(step).wait_send()
+        sib_copy(step).wait_send()
+
+    @pl.loop(1, 8)
+    def _(step):
+        z_copy(step).wait_send()
+
+
+def gathered(codes, node_scale, basis):
+    nodes, snaps = codes.shape
+    modes = basis.shape[1]
+    chunks = 8
+    dma = pltpu.SemaphoreType.DMA
+    out = pl.pallas_call(
+        gather_kernel,
+        out_shape=jax.ShapeDtypeStruct((256, 8, modes), jnp.float32),
+        in_specs=[
+            pl.BlockSpec(memory_space=pltpu.VMEM),
+            pl.BlockSpec(memory_space=pl.ANY),
+            pl.BlockSpec(memory_space=pl.ANY),
+        ],
+        out_specs=pl.BlockSpec(memory_space=pltpu.VMEM),
+        scratch_shapes=[
+            pltpu.VMEM((nodes, snaps), jnp.int32),
+            pltpu.VMEM((nodes, modes), jnp.bfloat16),
+            pltpu.VMEM((modes, snaps), jnp.float32),
+            pltpu.VMEM((16, 8, modes), jnp.float32),
+            pltpu.VMEM((16, 8, modes), jnp.float32),
+            dma((chunks,)), dma((chunks,)),
+            dma((16,)), dma((16,)), dma((8,)), dma((8,)), dma((16,)), dma((16,)), dma((16,)), dma((16,)),
+        ],
+        compiler_params=pltpu.CompilerParams(
+            collective_id=0, has_side_effects=True, vmem_limit_bytes=32 * 1024 * 1024
+        ),
+        name="project_and_gather",
+    )(node_scale.reshape(nodes // 128, 128), codes, basis)
+    return out.reshape(256 * 8, modes)
+
+
 def per_device(codes, node_scale, basis, regular, feature_order, panel_inverse):
     rank_count = basis.shape[1]
     snap_local = codes.shape[1]
@@ -60,20 +243,12 @@
     snap_total = snap_local * lax.axis_size("tm")
     panel_width = panel_inverse.shape[1]
     span = 2 * panel_width
-    scaled_basis = (basis.astype(jnp.float32) * node_scale[:, None]).astype(jnp.bfloat16)
-    code_values = codes.astype(jnp.bfloat16)
     row_offset = lax.axis_index("node") * row_size
     col_offset = lax.axis_index("tm") * col_size
     row_picks = selectors(lax.dynamic_slice_in_dim(feature_order, row_offset, row_size), rank_count)
     col_picks = selectors(lax.dynamic_slice_in_dim(feature_order, col_offset, col_size), rank_count)
     pan_picks = selectors(feature_order[:span], rank_count)
-    summed = lax.psum(
-        lax.dot_general(
-            code_values, scaled_basis, (((0,), (0,)), ((), ())), preferred_element_type=jnp.float32
-        ),
-        "node",
-    )
-    pieces = spread(lax.all_gather(summed, "tm", axis=0, tiled=True))
+    pieces = spread(gathered(codes, node_scale, basis))
     row_feats = make_features(pieces, row_picks)
     col_feats = make_features(pieces, col_picks)
     pan_feats = make_features(pieces, pan_picks)

time: 237 us -> 68.7 us (0.29)
  waiting for transfers between devices: 188 us -> 0 us
  Pallas kernels: 0 us -> 34.2 us
  between operations: 13.6 us -> 0.25 us
  matrix products: 28.9 us -> 25.1 us
  local copies, waits for them, and re-layouts: 2.42 us -> 5.95 us
    psum x1 -> x0, waiting for transfers between devices: 147 us -> none  [per_device(): lax.psum(lax.dot_general(code_values, scaled_basis, (((0,), (0,)), ((), (...]
    all_gather x1 -> x0, waiting for transfers between devices: 41.1 us -> none  [per_device(): pieces = spread(lax.all_gather(summed, 'tm', axis=0, tiled=True))]
    pallas_call x0 -> x1, Pallas kernels: none -> 34.2 us  [gathered(): pl.pallas_call(gather_kernel, out_shape=jax.ShapeDtypeStruct((256, 8, mod...]
    dot_general x1 -> x0, matrix products: 3.71 us -> none  [per_device(): lax.dot_general(code_values, scaled_basis, (((0,), (0,)), ((), ())), pref...]
    unnamed x8 -> x14, local copies, waits for them, and re-layouts: 0.01 us -> 3.55 us
  transfers between devices with their start and end apart: 2 -> 0, of which waited for: 2 -> 0; matrix products, arithmetic and copies ran while one was open for 2% -> 0% of each run, Pallas kernels for 0% -> 0%
where the time goes in v2:
time: 68.7 us; the launch traced here: 68.3 us
  Pallas kernels  34.2 us (50%)
  matrix products  25.1 us (37%)
  local copies, waits for them, and re-layouts  5.95 us (9%)
  other arithmetic  2.8 us (4%)
    pallas_call x1, Pallas kernels, gathered(): pl.pallas_call(gather_kernel, out_shape=jax.ShapeDtypeStruct((256, 8, mod...  34.2 us
    dot_general x6, matrix products, highest(): jnp.dot(left_mat, right_mat, precision=lax.Precision.HIGHEST, preferred_e...  14 us
    dot_general x4, matrix products, contract(): lax.dot_general(left_feats, right_feats, (((1,), (1,)), ((), ())), prefer...  6.41 us
    unnamed x14, local copies, waits for them, and re-layouts  3.55 us
    dot_general x3, matrix products, make_features(): lax.dot_general(trail, pieces, dims, preferred_element_type=jnp.float32)  2.46 us
    dot_general x3, matrix products, make_features(): lax.dot_general(lead, pieces, dims, preferred_element_type=jnp.float32)  2.29 us

profile of v2, /device:TPU:1, one launch (start us, length us, event | category | flops | bytes accessed | tf_op | source)
XLA Modules:
  0.0 68.3 jit_solution(8267258479995231673)
XLA Ops:
  0.0 0.9 %fusion.48 = (s32[524]{0:T(1024)S(1)}, s32[524]{0:T(1024)S(1)}, s32[524]{0:T(1024)S(1)}) fusion(s32[8384]{0:T(1024)} %param.19, s32[]{:T(128)S(6)} %select_n.19, s32[]{:T(128)S(6)} %select_n.17), kind=kLoop, calls=%fused_computation.80 | loop fusion | bytes 12584 | tf_op jit(solution)/shard_map/dynamic_slice | solution.py:249
  0.9 0.9 %compare_and_fusion = (pred[524,128]{1,0:T(8,128)(4,1)S(1)}, pred[524,128]{1,0:T(8,128)(4,1)S(1)}, pred[524,128]{1,0:T(8,128)(4,1)S(1)}) fusion(s32[128]{0:T(128)} %constant.33.clone, s32[128]{0:T(128)} %constant.32.clone, s32[524]{0:T(1024)S(1)} %get-tuple-element.22, s32[524]{0:T(1024)S(1)} %get-tuple-element.20, s32[524]{0:T(1024)S(1)} %get-tuple-element.21), kind=kLoop, calls=%fused_computation.61 | loop fusion | flops 603648 | bytes 208528 | tf_op jit(solution)/shard_map/and | solution.py:22
  1.8 1.6 %copy-done = s32[4096,128]{1,0:T(8,128)S(1)} copy-done((s32[4096,128]{1,0:T(8,128)S(1)}, s32[4096,128]{1,0:T(8,128)}, u32[]{:S(2)}) %copy-start) | copy-done | bytes 2097176
  3.4 1.2 %copy-done.1 = bf16[4096,128]{1,0:T(8,128)(2,1)S(1)} copy-done((bf16[4096,128]{1,0:T(8,128)(2,1)S(1)}, bf16[4096,128]{1,0:T(8,128)(2,1)}, u32[]{:S(2)}) %copy-start.1) | copy-done | bytes 1048600
  4.6 0.7 %copy-done.2 = f32[4096]{0:T(1024)S(1)} copy-done((f32[4096]{0:T(1024)S(1)}, f32[4096]{0:T(1024)}, u32[]{:S(2)}) %copy-start.2) | copy-done | bytes 16408
  5.4 34.2 %project_and_gather.1 = f32[256,8,128]{2,1,0:T(8,128)S(1)} custom-call(f32[32,128]{1,0:T(8,128)S(1)} %bitcast.22, s32[4096,128]{1,0:T(8,128)S(1)} %copy-done, bf16[4096,128]{1,0:T(8,128)(2,1)S(1)} %copy-done.1), custom_call_target="tpu_custom_call" | custom-call | tf_op jit(solution)/shard_map/project_and_gather/pallas_call | solution.py:211
  39.8 0.8 %fusion.15 = f32[524,2048]{1,0:T(8,128)S(1)} fusion(pred[524,128]{1,0:T(8,128)(4,1)S(1)} %get-tuple-element.25, bf16[2048,128]{1,0:T(8,128)(2,1)S(1)} %get-tuple-element.15, bf16[2048,128]{1,0:T(8,128)(2,1)S(1)} %get-tuple-element.14), kind=kOutput, calls=%fused_computation.30 | convolution fusion | flops 551685120 | bytes 5408256 | tf_op jit(solution)/shard_map/dot_general | solution.py:41
  41.3 0.8 %multiply_convert_fusion.2 = bf16[524,2048]{1,0:T(8,128)(2,1)S(1)} fusion(f32[524,2048]{1,0:T(8,128)S(1)} %fusion.15, f32[524]{0:T(1024)S(1)} %get-tuple-element.26, pred[524,128]{1,0:T(8,128)(4,1)S(1)} %iota_compare_fusion.4, bf16[2048,128]{1,0:T(8,128)(2,1)S(1)} %get-tuple-element.15, bf16[2048,128]{1,0:T(8,128)(2,1)S(1)} %get-tuple-element.14), kind=kOutput, calls=%fused_computation.2 | convolution fusion | flops 554904576 | bytes 7556656 | tf_op jit(solution)/shard_map/dot_general | solution.py:42
  42.1 0.8 %fusion.22 = f32[524,2048]{1,0:T(8,128)S(1)} fusion(pred[524,128]{1,0:T(8,128)(4,1)S(1)} %get-tuple-element.24, bf16[2048,128]{1,0:T(8,128)(2,1)S(1)} %get-tuple-element.15, bf16[2048,128]{1,0:T(8,128)(2,1)S(1)} %get-tuple-element.14), kind=kOutput, calls=%fused_computation.37 | convolution fusion | flops 551685120 | bytes 5408256 | tf_op jit(solution)/shard_map/dot_general | solution.py:41
  43.0 0.8 %multiply_convert_fusion.1 = bf16[524,2048]{1,0:T(8,128)(2,1)S(1)} fusion(f32[524,2048]{1,0:T(8,128)S(1)} %fusion.22, f32[524]{0:T(1024)S(1)} %get-tuple-element.10, pred[524,128]{1,0:T(8,128)(4,1)S(1)} %iota_compare_fusion.3, bf16[2048,128]{1,0:T(8,128)(2,1)S(1)} %get-tuple-element.15, bf16[2048,128]{1,0:T(8,128)(2,1)S(1)} %get-tuple-element.14), kind=kOutput, calls=%fused_computation.1 | convolution fusion | flops 554904576 | bytes 7556656 | tf_op jit(solution)/shard_map/dot_general | solution.py:42
  43.9 0.9 %fusion.47 = (f32[524]{0:T(1024)S(1)}, f32[524]{0:T(1024)S(1)}) fusion(f32[8384]{0:T(1024)} %param.18, s32[]{:T(128)S(6)} %select_n.17), kind=kLoop, calls=%fused_computation.79 | loop fusion | bytes 8388 | tf_op jit(solution)/shard_map/slice | solution.py:266
  44.7 1.9 %fusion = f32[524,524]{1,0:T(8,128)S(1)} fusion(bf16[524,2048]{1,0:T(8,128)(2,1)S(1)} %multiply_convert_fusion.2, bf16[524,2048]{1,0:T(8,128)(2,1)S(1)} %multiply_convert_fusion.1, f32[524]{0:T(1024)S(1)} %get-tuple-element.19, s32[524]{0:T(1024)S(1)} %get-tuple-element.28, s32[524]{0:T(1024)S(1)} %get-tuple-element.29), kind=kOutput, calls=%fused_computation.9 | convolution fusion | flops 1125761536 | bytes 5397200 | tf_op jit(solution)/shard_map/dot_general | solution.py:47
  46.6 0.8 %fusion.29 = f32[524,2048]{1,0:T(8,128)S(1)} fusion(pred[524,128]{1,0:T(8,128)(4,1)S(1)} %get-tuple-element.23, bf16[2048,128]{1,0:T(8,128)(2,1)S(1)} %get-tuple-element.15, bf16[2048,128]{1,0:T(8,128)(2,1)S(1)} %get-tuple-element.14), kind=kOutput, calls=%fused_computation.44 | convolution fusion | flops 551685120 | bytes 5408256 | tf_op jit(solution)/shard_map/dot_general | solution.py:41
  47.4 0.7 %convert_subtract_fusion = (f32[524]{0:T(1024)S(1)}, s32[524]{0:T(1024)S(1)}) fusion(s32[524]{0:T(1024)S(1)} %get-tuple-element.5, s32[8384]{0:T(1024)} %param.19), kind=kLoop, calls=%fused_computation.64 | loop fusion | flops 2096 | bytes 8384 | tf_op jit(solution)/shard_map/sub | solution.py:27
  48.2 0.8 %multiply_convert_fusion = bf16[524,2048]{1,0:T(8,128)(2,1)S(1)} fusion(f32[524,2048]{1,0:T(8,128)S(1)} %fusion.29, f32[524]{0:T(1024)S(1)} %get-tuple-element.8, pred[524,128]{1,0:T(8,128)(4,1)S(1)} %iota_compare_fusion.2, bf16[2048,128]{1,0:T(8,128)(2,1)S(1)} %get-tuple-element.15, bf16[2048,128]{1,0:T(8,128)(2,1)S(1)} %get-tuple-element.14), kind=kOutput, calls=%fused_computation | convolution fusion | flops 554904576 | bytes 7556656 | tf_op jit(solution)/shard_map/dot_general | solution.py:42
  49.1 1.9 %fusion.1 = f32[524,524]{1,0:T(8,128)S(1)} fusion(bf16[524,2048]{1,0:T(8,128)(2,1)S(1)} %multiply_convert_fusion.2, bf16[524,2048]{1,0:T(8,128)(2,1)S(1)} %multiply_convert_fusion, f32[524]{0:T(1024)S(1)} %get-tuple-element.19, s32[524]{0:T(1024)S(1)} %get-tuple-element.29), kind=kOutput, calls=%fused_computation.10 | convolution fusion | flops 1125761536 | bytes 5395104 | tf_op jit(solution)/shard_map/dot_general | solution.py:47
  51.6 1.6 %fusion.13 = f32[524,262]{0,1:T(8,128)S(1)} fusion(f32[524,524]{1,0:T(8,128)S(1)} %fusion.1, f32[1,262,262]{2,0,1:T(1,128)S(1)} %get-tuple-element.17), kind=kOutput, calls=%fused_computation.28 | convolution fusion | flops 431633472 | bytes 1762592 | tf_op jit(solution)/shard_map/dot_general | solution.py:53
  53.2 0.8 %convolution_multiply_fusion.3 = f32[262,262]{1,0:T(8,128)S(1)} fusion(bf16[524,2048]{1,0:T(8,128)(2,1)S(1)} %multiply_convert_fusion), kind=kOutput, calls=%fused_computation.22 | convolution fusion | flops 281234464 | bytes 2420880 | tf_op jit(solution)/shard_map/dot_general | solution.py:47
  54.0 2.2 %convolution_subtract_fusion.1 = f32[524,262]{1,0:T(8,128)S(1)} fusion(f32[524,262]{0,1:T(8,128)S(1)} %fusion.13, f32[262,262]{1,0:T(8,128)S(1)} %convolution_multiply_fusion.3, f32[524,524]{1,0:T(8,128)S(1)} %fusion.1), kind=kOutput, calls=%fused_computation.20 | convolution fusion | flops 431770752 | bytes 1922032 | tf_op jit(solution)/shard_map/dot_general | solution.py:53
  56.2 1.6 %fusion.36 = f32[524,262]{0,1:T(8,128)S(1)} fusion(f32[524,262]{1,0:T(8,128)S(1)} %convolution_subtract_fusion.1, f32[1,262,262]{2,0,1:T(1,128)S(1)} %get-tuple-element.16), kind=kOutput, calls=%fused_computation.52 | convolution fusion | flops 431633472 | bytes 1372880 | tf_op jit(solution)/shard_map/dot_general | solution.py:53
  57.8 1.9 %fusion.37 = f32[262,262]{1,0:T(8,128)S(1)} fusion(f32[262,262]{1,0:T(8,128)S(1)} %convolution_multiply_fusion.3, f32[1,262,262]{2,0,1:T(1,128)S(1)} %get-tuple-element.17), kind=kOutput, calls=%fused_computation.54 | convolution fusion | flops 215816736 | bytes 823728 | tf_op jit(solution)/shard_map/dot_general | solution.py:53
  59.7 1.9 %fusion.2 = f32[524,524]{1,0:T(8,128)S(1)} fusion(bf16[524,2048]{1,0:T(8,128)(2,1)S(1)} %multiply_convert_fusion, bf16[524,2048]{1,0:T(8,128)(2,1)S(1)} %multiply_convert_fusion.1, f32[524]{0:T(1024)S(1)} %get-tuple-element.18, s32[524]{0:T(1024)S(1)} %get-tuple-element.28), kind=kOutput, calls=%fused_computation.11 | convolution fusion | flops 1125761536 | bytes 5395104 | tf_op jit(solution)/shard_map/dot_general | solution.py:47
  61.6 1.5 %convolution_subtract_fusion.2 = f32[262,524]{1,0:T(8,128)S(1)} fusion(f32[262,262]{1,0:T(8,128)S(1)} %fusion.37, f32[524,524]{1,0:T(8,128)S(1)} %fusion.2), kind=kOutput, calls=%fused_computation.21 | convolution fusion | flops 431770752 | bytes 1922032 | tf_op jit(solution)/shard_map/dot_general | solution.py:53
  63.1 5.2 %convolution_subtract_fusion = f32[524,524]{1,0:T(8,128)} fusion(f32[524,524]{1,0:T(8,128)S(1)} %fusion, f32[524,262]{0,1:T(8,128)S(1)} %fusion.36, f32[524,262]{0,1:T(8,128)S(1)} %fusion.13, f32[262,524]{1,0:T(8,128)S(1)} %convolution_subtract_fusion.2, f32[262,524]{1,0:T(8,128)S(1)} %slice.46), kind=kOutput, calls=%fused_computation.5 | convolution fusion | flops 1727357696 | bytes 4393216 | tf_op jit(solution)/shard_map/dot_general | solution.py:53
  (20 shorter events, 1.9 us)
Async XLA Ops:
  1.8 1.6 %copy-start = (s32[4096,128]{1,0:T(8,128)S(1)}, s32[4096,128]{1,0:T(8,128)}, u32[]{:S(2)}) copy-start(s32[4096,128]{1,0:T(8,128)} %codes_hbm.1) | copy-start | bytes 6291460
  3.4 1.2 %copy-start.1 = (bf16[4096,128]{1,0:T(8,128)(2,1)S(1)}, bf16[4096,128]{1,0:T(8,128)(2,1)}, u32[]{:S(2)}) copy-start(bf16[4096,128]{1,0:T(8,128)(2,1)} %basis_hbm.1) | copy-start | bytes 3145732
  4.6 0.7 %copy-start.2 = (f32[4096]{0:T(1024)S(1)}, f32[4096]{0:T(1024)}, u32[]{:S(2)}) copy-start(f32[4096]{0:T(1024)} %param.16) | copy-start | bytes 49156
  39.7 0.8 %copy-start.4 = (s32[128]{0:T(128)S(1)}, s32[128]{0:T(128)}, u32[]{:S(2)}) copy-start(s32[128]{0:T(128)} %constant.33.clone) | copy-start | bytes 1540
  39.7 0.8 %copy-start.5 = (s32[128]{0:T(128)S(1)}, s32[128]{0:T(128)}, u32[]{:S(2)}) copy-start(s32[128]{0:T(128)} %constant.32.clone) | copy-start | bytes 1540
  39.8 0.8 %copy-start.6 = (s32[128]{0:T(128)S(1)}, s32[128]{0:T(128)}, u32[]{:S(2)}) copy-start(s32[128]{0:T(128)} %constant.35) | copy-start | bytes 1540
  49.1 1.9 %copy-start.3 = (f32[2,262,262]{2,0,1:T(2,128)S(1)}, f32[2,262,262]{2,0,1:T(2,128)}, u32[]{:S(2)}) copy-start(f32[2,262,262]{2,0,1:T(2,128)} %param.20) | copy-start | bytes 1647460

commit v3 on v1

v3 whole, which is shorter than its diff:
```python
import jax
import jax.numpy as jnp
from jax import lax
from jax.experimental import pallas as pl
from jax.experimental.pallas import tpu as pltpu
from jax.sharding import PartitionSpec as P

MESH = pl.DeviceIdType.MESH
F32, BF16 = jnp.float32, jnp.bfloat16
ROWS = 528
COLS = 640
WIDE = 384
TALL = 272
COL_AT, FIRST_AT, SECOND_AT = COLS, 2 * COLS, 2 * COLS + WIDE
ALL = 2 * COLS + 2 * WIDE


def nt(left, right):
    return lax.dot_general(left, right, (((1,), (1,)), ((), ())), preferred_element_type=F32)


def nn(left, right):
    return lax.dot_general(left, right, (((1,), (0,)), ((), ())), preferred_element_type=F32)


def halves(values):
    high = values.astype(BF16)
    return high, (values - high.astype(F32)).astype(BF16)


def thrice(dot, left, right):
    return dot(left[0], right[0]) + dot(left[0], right[1]) + dot(left[1], right[0])


def kernel(
    order_ref, regular_ref, scale_ref, panel_ref, codes_hbm, basis_hbm, out_ref,
    codes_buf, basis_buf, partial, slots, table, lead, trail, constant, feats,
    row_acc, first_acc, second_acc, cross_acc, inv_high, inv_low,
    code_sem, basis_sem, rs_send, rs_recv, z_send, z_recv, xy_send, xy_recv, sib_send, sib_recv,
):
    node, tm = lax.axis_index("node"), lax.axis_index("tm")
    x, z_hi = node // 4, node % 4
    z_lo, y, core = tm // 8, (tm // 2) % 4, tm % 2
    z = z_hi * 2 + z_lo
    modes = basis_buf.shape[1]
    width = panel_ref.shape[0]
    size = out_ref.shape[0]

    def place(at_x, at_y, at_z, at_core):
        return (at_x * 4 + at_z // 2, (at_z % 2) * 8 + at_y * 2 + at_core)

    def node_peer(step):
        return ((node + step) % 16, tm)

    def z_peer(step):
        return place(x, y, (z + step) % 8, core)

    def xy_peer(step):
        return place((x + step // 4) % 4, (y + step % 4) % 4, z, core)

    sibling = place(x, y, z, 1 - core)
    block = (x * 4 + y) * 2 + core

    def rs_copy(step):
        peer = node_peer(step)
        return pltpu.make_async_remote_copy(
            src_ref=partial.at[peer[0]], dst_ref=slots.at[step],
            send_sem=rs_send.at[step], recv_sem=rs_recv.at[step],
            device_id=peer, device_id_type=MESH,
        )

    def z_copy(step):
        piece = table.at[block, pl.ds(z * 8, 8)]
        return pltpu.make_async_remote_copy(
            src_ref=piece, dst_ref=piece, send_sem=z_send.at[step], recv_sem=z_recv.at[step],
            device_id=z_peer(step), device_id_type=MESH,
        )

    def xy_copy(step):
        return pltpu.make_async_remote_copy(
            src_ref=table.at[block], dst_ref=table.at[block],
            send_sem=xy_send.at[step], recv_sem=xy_recv.at[step],
            device_id=xy_peer(step), device_id_type=MESH,
        )

    def sib_copy(step):
        from_x, from_y = (x + 4 - step // 4) % 4, (y + 4 - step % 4) % 4
        at = (from_x * 4 + from_y) * 2 + core
        return pltpu.make_async_remote_copy(
            src_ref=table.at[at], dst_ref=table.at[at],
            send_sem=sib_send.at[step], recv_sem=sib_recv.at[step],
            device_id=sibling, device_id_type=MESH,
        )

    chunks = code_sem.shape[0]
    rows = codes_buf.shape[0] // chunks

    def fetch(chunk):
        part = pl.ds(chunk * rows, rows)
        return (
            pltpu.make_async_copy(codes_hbm.at[part], codes_buf.at[part], code_sem.at[chunk]),
            pltpu.make_async_copy(basis_hbm.at[part], basis_buf.at[part], basis_sem.at[chunk]),
        )

    for chunk in range(chunks):
        for copy in fetch(chunk):
            copy.start()

    barrier = pltpu.get_barrier_semaphore()

    def greet(peer):
        pl.semaphore_signal(barrier, inc=1, device_id=peer, device_id_type=MESH)

    @pl.loop(1, 16)
    def _(step):
        greet(node_peer(step))
        greet(xy_peer(step))

    @pl.loop(1, 8)
    def _(step):
        greet(z_peer(step))

    greet(sibling)

    total = jnp.zeros((modes, codes_buf.shape[1]), F32)
    for chunk in range(chunks):
        for copy in fetch(chunk):
            copy.wait()
        turned = []
        for piece in range(rows // 128):
            row = chunk * (rows // 128) + piece
            basis = basis_buf[pl.ds(row * 128, 128), :].astype(F32)
            turned.append((basis.T * scale_ref[row : row + 1, :]).astype(BF16))
        values = codes_buf[pl.ds(chunk * rows, rows), :].astype(F32).astype(BF16)
        total = total + nn(jnp.concatenate(turned, axis=1), values)
    partial[...] = total.T.reshape(partial.shape)

    pl.semaphore_wait(barrier, 38)

    @pl.loop(1, 16)
    def _(step):
        rs_copy(step).start()

    mode = lax.broadcasted_iota(jnp.int32, (128, 128), 1)
    start = mode * (modes + 1) - mode * (mode - 1) // 2

    @pl.loop(0, ALL // 128)
    def _(at):
        chosen = jnp.broadcast_to(order_ref[pl.ds(at, 1), :], (128, 128)).T.astype(jnp.int32)
        among = jnp.logical_and(chosen >= start, chosen < start + (modes + 1 - mode))
        shift = jnp.sum(jnp.where(among, (mode - start).astype(F32), 0.0), axis=1, keepdims=True)
        trailing = chosen + jnp.broadcast_to(shift, (128, 128)).astype(jnp.int32)
        part = pl.ds(at * 128, 128)
        among = jnp.where(among, 1.0, 0.0).astype(BF16)
        lead[part, 0:128] = among
        lead[part, 128:256] = among
        same = jnp.where(trailing == mode, 1.0, 0.0).astype(BF16)
        trail[part, 0:128] = same
        trail[part, 128:256] = same
        constant[part, :] = jnp.where(trailing == modes, 1.0, 0.0)

    feats[...] = jnp.zeros_like(feats)
    row_acc[...] = jnp.zeros_like(row_acc)
    first_acc[...] = jnp.zeros_like(first_acc)
    second_acc[...] = jnp.zeros_like(second_acc)
    cross_acc[...] = jnp.zeros_like(cross_acc)
    inv_high[...] = jnp.zeros_like(inv_high)
    inv_low[...] = jnp.zeros_like(inv_low)
    for panel in range(2):
        high, low = halves(panel_ref[:, panel, :])
        inv_high[panel, 0:width, 0:width] = high
        inv_low[panel, 0:width, 0:width] = low

    @pl.loop(1, 16)
    def _(step):
        rs_copy(step).wait_recv()

    summed = partial[node]
    for step in range(1, 16):
        summed = summed + slots[step]
    table[block, pl.ds(z * 8, 8), :] = summed

    @pl.loop(1, 8)
    def _(step):
        z_copy(step).start()

    @pl.loop(1, 8)
    def _(step):
        z_copy(step).wait_recv()

    for step in (1, 3, 2, 4, 5, 7, 6, 12, 13, 15, 14, 8, 9, 11, 10):
        xy_copy(step).start()
    sib_copy(0).start()
    for step in (1, 3, 2):
        xy_copy(step).wait_recv()
        sib_copy(step).start()
    for step in range(4):
        sib_copy(step).wait_recv()

    for turn, plane in enumerate((0, 1, 3, 2)):
        snaps = 8 * table.shape[1]
        values = table[pl.ds(((x + 4 - plane) % 4) * 8, 8)].reshape(snaps, modes)
        pieces = jnp.concatenate(halves(values), axis=1)
        for low, count in ((0, ROWS), (COL_AT, ROWS), (FIRST_AT, TALL), (SECOND_AT, TALL)):
            part = slice(low, low + count)
            once = jnp.concatenate([constant[part, :]] * (snaps // 128), axis=1)
            product = nt(lead[part, :], pieces) * (nt(trail[part, :], pieces) + once)
            feats[part, :] = product.astype(BF16)
        if turn < 3:
            after = (0, 1, 3, 2)[turn + 1]
            for step in (0, 1, 3, 2):
                xy_copy(after * 4 + step).wait_recv()
                sib_copy(after * 4 + step).start()
        columns = feats[COL_AT:FIRST_AT, :]
        row_acc[...] += nt(feats[0:ROWS, :], feats[COL_AT:ALL, :])
        first_acc[0:TALL, :] += nt(feats[FIRST_AT : FIRST_AT + TALL, :], columns)
        second = feats[SECOND_AT : SECOND_AT + TALL, :]
        second_acc[0:TALL, :] += nt(second, columns)
        cross_acc[0:TALL, :] += nt(second, feats[FIRST_AT:SECOND_AT, :])
        if turn < 3:
            for step in range(4):
                sib_copy(after * 4 + step).wait_recv()

    sib_copy(0).wait_send()

    @pl.loop(1, 16)
    def _(step):
        rs_copy(step).wait_send()
        xy_copy(step).wait_send()
        sib_copy(step).wait_send()

    @pl.loop(1, 8)
    def _(step):
        z_copy(step).wait_send()

    share = 1.0 / (table.shape[0] * table.shape[1])

    def diagonal(row_from, col_from, height, length, at):
        row = lax.broadcasted_iota(jnp.int32, (height, length), 0) + row_from
        col = lax.broadcasted_iota(jnp.int32, (height, length), 1) + col_from
        return jnp.where(row == col, regular_ref[0:1, at : at + length], 0.0)

    row_from, col_from = node * size, tm * size
    first_left = row_acc[:, COLS : COLS + WIDE] * share + diagonal(row_from, 0, ROWS, WIDE, COLS)
    second_left = row_acc[:, COLS + WIDE :] * share + diagonal(row_from, width, ROWS, WIDE, COLS + WIDE)
    first_up = halves(first_acc[...] * share + diagonal(0, col_from, WIDE, COLS, 0))
    second_up = second_acc[...] * share + diagonal(width, col_from, WIDE, COLS, 0)
    cross = halves(cross_acc[...] * share)
    first_inv = (inv_high[0], inv_low[0])
    second_inv = (inv_high[1], inv_low[1])
    first_left = halves(thrice(nn, halves(first_left), first_inv))
    second_left = second_left - thrice(nt, first_left, cross)
    second_left = halves(thrice(nn, halves(second_left), second_inv))
    second_up = halves(second_up - thrice(nn, halves(thrice(nn, cross, first_inv)), first_up))
    result = row_acc[:, 0:COLS] * share + diagonal(row_from, col_from, ROWS, COLS, 0)
    result = result - thrice(nn, first_left, first_up) - thrice(nn, second_left, second_up)
    out_ref[...] = result[0:size, 0:size]


def per_device(codes, node_scale, basis, regular, feature_order, panel_inverse):
    nodes, snaps = codes.shape
    modes = basis.shape[1]
    size = regular.shape[0] // lax.axis_size("node")
    width = panel_inverse.shape[1]
    row_from, col_from = lax.axis_index("node") * size, lax.axis_index("tm") * size

    def pick(values, low, count, length, fill):
        taken = lax.dynamic_slice_in_dim(values, low, count)
        return jnp.pad(taken, (0, length - count), constant_values=fill)

    order = feature_order.astype(F32)
    order = jnp.concatenate([
        pick(order, row_from, size, COLS, -1.0), pick(order, col_from, size, COLS, -1.0),
        pick(order, 0, width, WIDE, -1.0), pick(order, width, width, WIDE, -1.0),
    ]).reshape(ALL // 128, 128)
    diagonal = jnp.concatenate([
        pick(regular, col_from, size, COLS, 0.0),
        pick(regular, 0, width, WIDE, 0.0), pick(regular, width, width, WIDE, 0.0),
    ]).reshape(1, COLS + 2 * WIDE)
    chunks = 8
    dma = pltpu.SemaphoreType.DMA
    vmem = pl.BlockSpec(memory_space=pltpu.VMEM)
    hbm = pl.BlockSpec(memory_space=pltpu.HBM)
    return pl.pallas_call(
        kernel,
        out_shape=jax.ShapeDtypeStruct((size, size), F32),
        in_specs=[vmem, vmem, vmem, vmem, hbm, hbm],
        out_specs=vmem,
        scratch_shapes=[
            pltpu.VMEM((nodes, snaps), jnp.int32),
            pltpu.VMEM((nodes, modes), BF16),
            pltpu.VMEM((16, 8, modes), F32),
            pltpu.VMEM((16, 8, modes), F32),
            pltpu.VMEM((32, 64, modes), F32),
            pltpu.VMEM((ALL, 2 * modes), BF16),
            pltpu.VMEM((ALL, 2 * modes), BF16),
            pltpu.VMEM((ALL, 128), F32),
            pltpu.VMEM((ALL, 512), BF16),
            pltpu.VMEM((ROWS, COLS + 2 * WIDE), F32),
            pltpu.VMEM((WIDE, COLS), F32),
            pltpu.VMEM((WIDE, COLS), F32),
            pltpu.VMEM((WIDE, WIDE), F32),
            pltpu.VMEM((2, WIDE, WIDE), BF16),
            pltpu.VMEM((2, WIDE, WIDE), BF16),
            dma((chunks,)), dma((chunks,)),
            dma((16,)), dma((16,)), dma((8,)), dma((8,)), dma((16,)), dma((16,)), dma((16,)), dma((16,)),
        ],
        compiler_params=pltpu.CompilerParams(
            collective_id=0, has_side_effects=True, vmem_limit_bytes=56 * 1024 * 1024
        ),
        name="reduced_operators",
    )(
        order, diagonal, node_scale.reshape(nodes // 128, 128),
        jnp.transpose(panel_inverse, (1, 0, 2)), codes, basis,
    )


def solution(mesh):
    placed = (P("node", "tm"), P("node"), P("node", None), P(), P(), P())
    return jax.shard_map(
        per_device, mesh=mesh, in_specs=placed, out_specs=P("node", "tm"), check_vma=False
    )
```

time: 237 us -> 59.8 us (0.25)
  waiting for transfers between devices: 188 us -> 0 us
  Pallas kernels: 0 us -> 52.6 us
  matrix products: 28.9 us -> 0 us
  between operations: 13.6 us -> 0.01 us
    psum x1 -> x0, waiting for transfers between devices: 147 us -> none  [per_device(): lax.psum(lax.dot_general(code_values, scaled_basis, (((0,), (0,)), ((), (...]
    pallas_call x0 -> x1, Pallas kernels: none -> 52.6 us  [per_device(): pl.pallas_call(kernel, out_shape=jax.ShapeDtypeStruct((size, size), F32),...]
    all_gather x1 -> x0, waiting for transfers between devices: 41.1 us -> none  [per_device(): pieces = spread(lax.all_gather(summed, 'tm', axis=0, tiled=True))]
    dot_general x17 -> x0, matrix products: 28.9 us -> none  [the longest x6 14 us: highest(): jnp.dot(left_mat, right_mat, precision=lax.Precision.HIGHEST, preferred_e...]
    unnamed x8 -> x1, local copies, waits for them, and re-layouts: 0.01 us -> 2.49 us
  transfers between devices with their start and end apart: 2 -> 0, of which waited for: 2 -> 0; matrix products, arithmetic and copies ran while one was open for 2% -> 0% of each run, Pallas kernels for 0% -> 0%
where the time goes in v3:
time: 59.8 us; the launch traced here: 59.5 us
  Pallas kernels  52.6 us (88%)
  local copies, waits for them, and re-layouts  4.77 us (8%)
  other arithmetic  2.09 us (3%)
    pallas_call x1, Pallas kernels, per_device(): pl.pallas_call(kernel, out_shape=jax.ShapeDtypeStruct((size, size), F32),...  52.6 us
    unnamed x1, local copies, waits for them, and re-layouts  2.49 us
    dynamic_slice x4, local copies, waits for them, and re-layouts, pick(): taken = lax.dynamic_slice_in_dim(values, low, count)  1.68 us

profile of v3, /device:TPU:1, one launch (start us, length us, event | category | flops | bytes accessed | tf_op | source)
XLA Modules:
  0.0 59.5 jit_solution(7639022682672633462)
XLA Ops:
  0.0 0.8 %dynamic_slice.21 = f32[262]{0:T(512)S(1)} slice(f32[8384]{0:T(1024)} %param.9), slice={[262:524]} | slice | bytes 2096 | tf_op jit(solution)/shard_map/dynamic_slice | solution.py:268
  0.8 0.8 %dynamic_slice.20 = f32[524]{0:T(1024)S(1)} dynamic-slice(f32[8384]{0:T(1024)} %param.9, s32[]{:T(128)S(6)} %select_n.8), dynamic_slice_sizes={524} | dynamic-slice | bytes 4196 | tf_op jit(solution)/shard_map/dynamic_slice | solution.py:268
  1.5 0.8 %convert_element_type.3 = f32[8384]{0:T(1024)S(1)} convert(s32[8384]{0:T(1024)} %param.10) | non-fusion elementwise | flops 8384 | bytes 67072 | tf_op jit(solution)/shard_map/convert_element_type | solution.py:271
  2.3 0.1 dynamic_slice.22
  2.4 0.7 %slice_select_fusion.1 = (f32[384]{0:T(512)S(1)}, f32[384]{0:T(512)S(1)}) fusion(pred[384]{0:T(512)(128)(4,1)} %constant.18.clone.1, f32[8384]{0:T(1024)} %param.9, f32[8384]{0:T(1024)S(1)} %convert_element_type.3), kind=kLoop, calls=%fused_computation.14 | loop fusion | flops 768 | bytes 6528 | tf_op jit(solution)/shard_map/jit(_pad)/pad | solution.py:269
  3.1 0.1 fusion.3
  3.2 0.6 %fusion.order_ref = f32[16,128]{1,0:T(8,128)} fusion(f32[262]{0:T(512)S(1)} %dynamic_slice.22, f32[524]{0:T(1024)S(1)} %get-tuple-element.6, f32[524]{0:T(1024)S(1)} %get-tuple-element.5, f32[384]{0:T(512)S(1)} %get-tuple-element.8), kind=kLoop, calls=%fused_computation.7 | loop fusion | flops 22528 | bytes 14968 | tf_op jit(solution)/shard_map/reshape | solution.py:275
  3.8 0.6 %reshape.10.regular_ref = f32[1,1408]{1,0:T(1,128)} reshape(f32[1408]{0:T(1024)S(1)} %select_maximum_fusion) | data formatting | bytes 11264 | tf_op jit(solution)/shard_map/reshape | solution.py:279
  4.4 52.6 %reduced_operators.1 = f32[524,524]{1,0:T(8,128)} custom-call(f32[16,128]{1,0:T(8,128)} %fusion.order_ref, f32[1,1408]{1,0:T(1,128)} %reshape.10.regular_ref, f32[32,128]{1,0:T(8,128)} %bitcast.5, f32[262,2,262]{2,1,0:T(2,128)} %bitcast.4, s32[4096,128]{1,0:T(8,128)} %codes_hbm.1, bf16[4096,128]{1,0:T(8,128)(2,1)} %basis_hbm.1), custom_call_target="tpu_custom_call" | custom-call | tf_op jit(solution)/shard_map/reduced_operators/pallas_call | solution.py:284
  57.0 2.5 %copy.8 = f32[524,524]{1,0:T(8,128)} copy(f32[524,524]{1,0:T(8,128)} %reduced_operators.1) | data formatting | bytes 2196608
  (1 shorter events, 0.0 us)

commit v4 on v3

v4 whole, which is shorter than its diff:
```python
import jax
import jax.numpy as jnp
from jax import lax
from jax.experimental import pallas as pl
from jax.experimental.pallas import tpu as pltpu
from jax.sharding import PartitionSpec as P

MESH = pl.DeviceIdType.MESH
F32, BF16 = jnp.float32, jnp.bfloat16
ROWS = 528
COLS = 640
WIDE = 384
TALL = 272
COL_AT, FIRST_AT, SECOND_AT = COLS, 2 * COLS, 2 * COLS + WIDE
ALL = 2 * COLS + 2 * WIDE


def nt(left, right):
    return lax.dot_general(left, right, (((1,), (1,)), ((), ())), preferred_element_type=F32)


def nn(left, right):
    return lax.dot_general(left, right, (((1,), (0,)), ((), ())), preferred_element_type=F32)


def halves(values):
    high = values.astype(BF16)
    return high, (values - high.astype(F32)).astype(BF16)


def thrice(dot, left, right):
    return dot(left[0], right[0]) + dot(left[0], right[1]) + dot(left[1], right[0])


def kernel(
    order_hbm, regular_hbm, scale_hbm, panel_hbm, codes_hbm, basis_hbm, left_ref, up_ref, out_ref,
    codes_buf, basis_buf, scale_buf, order_buf, regular_buf, panel_buf, lines, order, regular,
    partial, slots, table, lead, trail, constant, feats,
    row_acc, up_acc, cross_acc, inv_high, inv_low,
    code_sem, basis_sem, small_sem, rs_send, rs_recv, one_send, one_recv, two_send, two_recv, sib_send, sib_recv,
):
    node, tm = lax.axis_index("node"), lax.axis_index("tm")
    x, z_hi = node // 4, node % 4
    z_lo, y, core = tm // 8, (tm // 2) % 4, tm % 2
    z = z_hi * 2 + z_lo
    inner, outer = y + core * (x - y), x + core * (y - x)
    modes = basis_buf.shape[1]
    width = panel_hbm.shape[0]
    size = out_ref.shape[0]

    def place(at_inner, at_outer, at_z, at_core):
        at_x = at_outer + core * (at_inner - at_outer)
        at_y = at_inner + core * (at_outer - at_inner)
        return (at_x * 4 + at_z // 2, (at_z % 2) * 8 + at_y * 2 + at_core)

    def node_peer(step):
        return ((node + step) % 16, tm)

    def one_peer(step):
        return place((inner + step // 8) % 4, outer, (z + step % 8) % 8, core)

    def two_peer(step):
        return place(inner, (outer + step) % 4, z, core)

    sibling = place(inner, outer, z, 1 - core)

    def rs_copy(step):
        peer = node_peer(step)
        return pltpu.make_async_remote_copy(
            src_ref=partial.at[peer[0]], dst_ref=slots.at[step],
            send_sem=rs_send.at[step], recv_sem=rs_recv.at[step],
            device_id=peer, device_id_type=MESH,
        )

    def one_copy(step):
        piece = table.at[core, outer, pl.ds((inner * 8 + z) * 8, 8)]
        return pltpu.make_async_remote_copy(
            src_ref=piece, dst_ref=piece, send_sem=one_send.at[step], recv_sem=one_recv.at[step],
            device_id=one_peer(step), device_id_type=MESH,
        )

    def two_copy(step):
        return pltpu.make_async_remote_copy(
            src_ref=table.at[core, outer], dst_ref=table.at[core, outer],
            send_sem=two_send.at[step], recv_sem=two_recv.at[step],
            device_id=two_peer(step), device_id_type=MESH,
        )

    def sib_copy(step):
        at = (outer + 4 - step) % 4
        return pltpu.make_async_remote_copy(
            src_ref=table.at[core, at], dst_ref=table.at[core, at],
            send_sem=sib_send.at[step], recv_sem=sib_recv.at[step],
            device_id=sibling, device_id_type=MESH,
        )

    chunks = code_sem.shape[0]
    rows = codes_buf.shape[0] // chunks

    def fetch(chunk):
        part = pl.ds(chunk * rows, rows)
        return (
            pltpu.make_async_copy(codes_hbm.at[part], codes_buf.at[part], code_sem.at[chunk]),
            pltpu.make_async_copy(basis_hbm.at[part], basis_buf.at[part], basis_sem.at[chunk]),
        )

    scale_copy = pltpu.make_async_copy(scale_hbm, scale_buf, small_sem.at[0])
    others = [
        pltpu.make_async_copy(order_hbm, order_buf, small_sem.at[1]),
        pltpu.make_async_copy(regular_hbm, regular_buf, small_sem.at[2]),
        pltpu.make_async_copy(panel_hbm, panel_buf, small_sem.at[3]),
    ]
    scale_copy.start()
    for chunk in range(chunks):
        for copy in fetch(chunk):
            copy.start()
    for copy in others:
        copy.start()

    barrier = pltpu.get_barrier_semaphore()

    def greet(peer):
        pl.semaphore_signal(barrier, inc=1, device_id=peer, device_id_type=MESH)

    @pl.loop(1, 16)
    def _(step):
        greet(node_peer(step))

    @pl.loop(1, 32)
    def _(step):
        greet(one_peer(step))

    @pl.loop(1, 4)
    def _(step):
        greet(two_peer(step))

    greet(sibling)

    total = jnp.zeros((modes, codes_buf.shape[1]), F32)
    scale_copy.wait()
    for chunk in range(chunks):
        for copy in fetch(chunk):
            copy.wait()
        turned = []
        for piece in range(rows // 128):
            row = chunk * (rows // 128) + piece
            basis = basis_buf[pl.ds(row * 128, 128), :].astype(F32)
            turned.append((basis.T * scale_buf[row : row + 1, :]).astype(BF16))
        values = codes_buf[pl.ds(chunk * rows, rows), :].astype(F32).astype(BF16)
        total = total + nn(jnp.concatenate(turned, axis=1), values)
    partial[...] = total.T.reshape(partial.shape)

    pl.semaphore_wait(barrier, 50)

    @pl.loop(1, 16)
    def _(step):
        rs_copy(step).start()

    for copy in others:
        copy.wait()
    row_from, col_from = node * size, tm * size
    lane = lax.broadcasted_iota(jnp.int32, (8, 128), 1)
    line = lax.broadcasted_iota(jnp.int32, (8, 128), 0)

    def unfold(flat, to_float):
        full = flat.shape[0] // 128
        for at in range(full):
            lines[at : at + 1, :] = to_float(flat[at * 128 : (at + 1) * 128].reshape(1, 128))
        rest = flat.shape[0] - full * 128
        lines[full : full + 1, 0:rest] = to_float(flat[full * 128 :].reshape(1, rest))

    def cut(low, count, height, fill):
        near = lines[pl.ds(low // 128, 8), :]
        shift = low % 128
        near = pltpu.roll(near, (128 - shift) % 128, 1)
        far = pltpu.roll(near, 7, 0)
        taken = jnp.where(lane < 128 - shift, near, far)
        return jnp.where(line * 128 + lane < count, taken, fill)[0:height]

    lines[64:80, :] = jnp.zeros((16, 128), F32)
    unfold(order_buf, lambda v: v.astype(F32))
    order[0:5, :] = cut(row_from, size, 5, -1.0)
    order[5:10, :] = cut(col_from, size, 5, -1.0)
    order[10:13, :] = cut(0, width, 3, -1.0)
    order[13:16, :] = cut(width, width, 3, -1.0)
    unfold(regular_buf, lambda v: v)
    regular[0:5, :] = cut(col_from, size, 5, 0.0)
    regular[5:8, :] = cut(0, width, 3, 0.0)
    regular[8:11, :] = cut(width, width, 3, 0.0)

    mode = lax.broadcasted_iota(jnp.int32, (128, 128), 1)
    start = mode * (modes + 1) - mode * (mode - 1) // 2

    @pl.loop(0, ALL // 128)
    def _(at):
        chosen = jnp.broadcast_to(order[pl.ds(at, 1), :], (128, 128)).T.astype(jnp.int32)
        among = jnp.logical_and(chosen >= start, chosen < start + (modes + 1 - mode))
        shift = jnp.sum(jnp.where(among, (mode - start).astype(F32), 0.0), axis=1, keepdims=True)
        trailing = chosen + jnp.broadcast_to(shift, (128, 128)).astype(jnp.int32)
        part = pl.ds(at * 128, 128)
        among = jnp.where(among, 1.0, 0.0).astype(BF16)
        lead[part, 0:128] = among
        lead[part, 128:256] = among
        same = jnp.where(trailing == mode, 1.0, 0.0).astype(BF16)
        trail[part, 0:128] = same
        trail[part, 128:256] = same
        constant[part, :] = jnp.where(trailing == modes, 1.0, 0.0)

    snapshots = 8 * table.shape[2]

    def diagonal(row_at, col_at, height, at):
        row = lax.broadcasted_iota(jnp.int32, (height, 128), 0) + row_at
        col = lax.broadcasted_iota(jnp.int32, (height, 128), 1) + col_at
        return jnp.where(row == col, regular[at : at + 1, :] * snapshots, 0.0)

    for at in range(11):
        part = slice(at * 128, at * 128 + 128)
        begin = col_from + at * 128 if at < 5 else (at - 5) * 128 if at < 8 else width + (at - 8) * 128
        row_acc[:, part] = diagonal(row_from, begin, ROWS, at)
        if at < 5:
            up_acc[0:WIDE, part] = diagonal(0, begin, WIDE, at)
            up_acc[WIDE:, part] = diagonal(width, begin, WIDE, at)
    cross_acc[...] = jnp.zeros_like(cross_acc)
    feats[...] = jnp.zeros_like(feats)
    inv_high[...] = jnp.zeros_like(inv_high)
    inv_low[...] = jnp.zeros_like(inv_low)
    for panel in range(2):
        high, low = halves(panel_buf[:, panel, :])
        inv_high[panel, 0:width, 0:width] = high
        inv_low[panel, 0:width, 0:width] = low

    @pl.loop(1, 16)
    def _(step):
        rs_copy(step).wait_recv()

    summed = partial[node]
    for step in range(1, 16):
        summed = summed + slots[step]
    table[core, outer, pl.ds((inner * 8 + z) * 8, 8), :] = summed

    @pl.loop(1, 32)
    def _(step):
        one_copy(step).start()

    @pl.loop(1, 32)
    def _(step):
        one_copy(step).wait_recv()

    for step in (1, 3, 2):
        two_copy(step).start()
    sib_copy(0).start()

    def own(step):
        return table[core, (outer + 4 - step) % 4]

    def other(step):
        return table[1 - core, (inner + 4 - step) % 4]

    def accumulate(first, second):
        values = jnp.concatenate([first, second], axis=0)
        pieces = jnp.concatenate(halves(values), axis=1)
        for low, count in ((0, ROWS), (COL_AT, ROWS), (FIRST_AT, TALL), (SECOND_AT, TALL)):
            part = slice(low, low + count)
            once = jnp.concatenate([constant[part, :]] * 4, axis=1)
            product = nt(lead[part, :], pieces) * (nt(trail[part, :], pieces) + once)
            feats[part, :] = product.astype(BF16)
        columns = feats[COL_AT:FIRST_AT, :]
        row_acc[...] += nt(feats[0:ROWS, :], feats[COL_AT:ALL, :])
        up_acc[0:TALL, :] += nt(feats[FIRST_AT : FIRST_AT + TALL, :], columns)
        later = feats[SECOND_AT : SECOND_AT + TALL, :]
        up_acc[WIDE : WIDE + TALL, :] += nt(later, columns)
        cross_acc[0:TALL, :] += nt(later, feats[FIRST_AT:SECOND_AT, :])

    sib_copy(0).wait_recv()
    accumulate(own(0), other(0))
    for step in (1, 3):
        two_copy(step).wait_recv()
        sib_copy(step).start()
    accumulate(own(1), own(3))
    two_copy(2).wait_recv()
    sib_copy(2).start()
    for step in (1, 3):
        sib_copy(step).wait_recv()
    accumulate(other(1), other(3))
    sib_copy(2).wait_recv()
    accumulate(own(2), other(2))

    share = 1.0 / snapshots
    first_inv = (inv_high[0], inv_low[0])
    second_inv = (inv_high[1], inv_low[1])
    cross = halves(cross_acc[...] * share)
    first_up = halves(up_acc[0:WIDE, :] * share)
    first_left = halves(row_acc[:, COLS : COLS + WIDE] * share)
    first_left = halves(thrice(nn, first_left, first_inv))
    second_left = row_acc[:, COLS + WIDE :] * share - thrice(nt, first_left, cross)
    second_left = thrice(nn, halves(second_left), second_inv)
    second_up = up_acc[WIDE:, :] * share - thrice(nn, halves(thrice(nn, cross, first_inv)), first_up)
    left_ref[:, 0:WIDE] = first_left[0][0:size]
    left_ref[:, WIDE:] = second_left[0:size].astype(BF16)
    up_ref[0:WIDE, :] = first_up[0][:, 0:size]
    up_ref[WIDE:, :] = second_up[:, 0:size].astype(BF16)
    out_ref[...] = row_acc[0:size, 0:size] * share

    @pl.loop(1, 16)
    def _(step):
        rs_copy(step).wait_send()

    @pl.loop(1, 32)
    def _(step):
        one_copy(step).wait_send()

    @pl.loop(1, 4)
    def _(step):
        two_copy(step).wait_send()

    @pl.loop(0, 4)
    def _(step):
        sib_copy(step).wait_send()


def per_device(codes, node_scale, basis, regular, feature_order, panel_inverse):
    nodes, snaps = codes.shape
    modes = basis.shape[1]
    size = regular.shape[0] // lax.axis_size("node")
    panels, width, _ = panel_inverse.shape
    chunks = 8
    dma = pltpu.SemaphoreType.DMA
    vmem = pl.BlockSpec(memory_space=pltpu.VMEM)
    hbm = pl.BlockSpec(memory_space=pltpu.HBM)
    left, up, matrix = pl.pallas_call(
        kernel,
        out_shape=(
            jax.ShapeDtypeStruct((size, 2 * WIDE), BF16),
            jax.ShapeDtypeStruct((2 * WIDE, size), BF16),
            jax.ShapeDtypeStruct((size, size), F32),
        ),
        in_specs=[hbm] * 6,
        out_specs=(vmem, vmem, vmem),
        scratch_shapes=[
            pltpu.VMEM((nodes, snaps), jnp.int32),
            pltpu.VMEM((nodes, modes), BF16),
            pltpu.VMEM((nodes // 128, 128), F32),
            pltpu.VMEM(feature_order.shape, jnp.int32),
            pltpu.VMEM(regular.shape, F32),
            pltpu.VMEM((width, panels, width), F32),
            pltpu.VMEM((80, 128), F32),
            pltpu.VMEM((16, 128), F32),
            pltpu.VMEM((16, 128), F32),
            pltpu.VMEM((16, 8, modes), F32),
            pltpu.VMEM((16, 8, modes), F32),
            pltpu.VMEM((2, 4, 256, modes), F32),
            pltpu.VMEM((ALL, 2 * modes), BF16),
            pltpu.VMEM((ALL, 2 * modes), BF16),
            pltpu.VMEM((ALL, 128), F32),
            pltpu.VMEM((ALL, 512), BF16),
            pltpu.VMEM((ROWS, COLS + 2 * WIDE), F32),
            pltpu.VMEM((2 * WIDE, COLS), F32),
            pltpu.VMEM((WIDE, WIDE), F32),
            pltpu.VMEM((2, WIDE, WIDE), BF16),
            pltpu.VMEM((2, WIDE, WIDE), BF16),
            dma((chunks,)), dma((chunks,)), dma((4,)),
            dma((16,)), dma((16,)), dma((32,)), dma((32,)), dma((4,)), dma((4,)), dma((4,)), dma((4,)),
        ],
        compiler_params=pltpu.CompilerParams(
            collective_id=0, has_side_effects=True, vmem_limit_bytes=40 * 1024 * 1024
        ),
        name="reduced_operators",
    )(*(
        pltpu.with_memory_space_constraint(each, pltpu.HBM)
        for each in (
            feature_order, regular, node_scale.reshape(nodes // 128, 128),
            jnp.transpose(panel_inverse, (1, 0, 2)), codes, basis,
        )
    ))
    return matrix - nn(left, up)


def solution(mesh):
    placed = (P("node", "tm"), P("node"), P("node", None), P(), P(), P())
    return jax.shard_map(
        per_device, mesh=mesh, in_specs=placed, out_specs=P("node", "tm"), check_vma=False
    )
```

time: 59.8 us -> 46.5 us (0.78)
  Pallas kernels: 52.6 us -> 44.5 us
  local copies, waits for them, and re-layouts: 4.77 us -> 0 us
  other arithmetic: 2.09 us -> 0 us
  matrix products: 0 us -> 1.9 us
    pallas_call x1, Pallas kernels: 52.6 us -> 44.5 us  [per_device(): pl.pallas_call(kernel, out_shape=(jax.ShapeDtypeStruct((size, 2 * WIDE),...]
    unnamed x1 -> x0, local copies, waits for them, and re-layouts: 2.49 us -> none
    dot_general x0 -> x1, matrix products: none -> 1.9 us  [nn(): lax.dot_general(left, right, (((1,), (0,)), ((), ())), preferred_element_...]
    dynamic_slice x4 -> x0, local copies, waits for them, and re-layouts: 1.68 us -> none  [pick(): taken = lax.dynamic_slice_in_dim(values, low, count)]
    convert_element_type x1 -> x0, other arithmetic: 0.77 us -> none  [per_device(): order = feature_order.astype(F32)]
    pad x1 -> x0, other arithmetic: 0.71 us -> none  [pick(): return jnp.pad(taken, (0, length - count), constant_values=fill)]
    reshape x1 -> x0, other arithmetic: 0.61 us -> none  [per_device(): order = jnp.concatenate([pick(order, row_from, size, COLS, -1.0), pick(or...]
    reshape x1 -> x0, local copies, waits for them, and re-layouts: 0.6 us -> none  [per_device(): diagonal = jnp.concatenate([pick(regular, col_from, size, COLS, 0.0), pic...]
where the time goes in v4:
time: 46.5 us; the launch traced here: 46.4 us
  Pallas kernels  44.5 us (96%)
  matrix products  1.9 us (4%)
    pallas_call x1, Pallas kernels, per_device(): pl.pallas_call(kernel, out_shape=(jax.ShapeDtypeStruct((size, 2 * WIDE),...  44.5 us
    dot_general x1, matrix products, nn(): lax.dot_general(left, right, (((1,), (0,)), ((), ())), preferred_element_...  1.9 us

profile of v4, /device:TPU:1, one launch (start us, length us, event | category | flops | bytes accessed | tf_op | source)
XLA Modules:
  0.0 46.4 jit_solution(170974322672131752)
XLA Ops:
  0.0 44.5 %reduced_operators.1 = (bf16[524,768]{1,0:T(8,128)(2,1)S(1)}, bf16[768,524]{1,0:T(8,128)(2,1)S(1)}, f32[524,524]{1,0:T(8,128)S(1)}) custom-call(s32[8384]{0:T(1024)} %order_hbm.1, f32[8384]{0:T(1024)} %regular_hbm.1, f32[32,128]{1,0:T(8,128)} %bitcast.5, f32[262,2,262]{2,1,0:T(2,128)} %bitcast.4, s32[4096,128]{1,0:T(8,128)} %codes_hbm.1, ...), custom_call_target="tpu_custom_call" | custom-call | tf_op jit(solution)/shard_map/reduced_operators/pallas_call | solution.py:330
  44.5 1.9 %convolution_subtract_fusion = f32[524,524]{1,0:T(8,128)} fusion(f32[524,524]{1,0:T(8,128)S(1)} %get-tuple-element.8, bf16[524,768]{1,0:T(8,128)(2,1)S(1)} %get-tuple-element.9, bf16[768,524]{1,0:T(8,128)(2,1)S(1)} %get-tuple-element.10), kind=kOutput, calls=%fused_computation | convolution fusion | flops 422023296 | bytes 3806336 | tf_op jit(solution)/shard_map/dot_general | solution.py:23

commit v5 on v4

--- a/solution.py
+++ b/solution.py
@@ -37,32 +37,34 @@
     codes_buf, basis_buf, scale_buf, order_buf, regular_buf, panel_buf, lines, order, regular,
     partial, slots, table, lead, trail, constant, feats,
     row_acc, up_acc, cross_acc, inv_high, inv_low,
-    code_sem, basis_sem, small_sem, rs_send, rs_recv, one_send, one_recv, two_send, two_recv, sib_send, sib_recv,
+    code_sem, basis_sem, small_sem, rs_send, rs_recv, z_send, z_recv, xy_send, xy_recv, sib_send, sib_recv,
 ):
     node, tm = lax.axis_index("node"), lax.axis_index("tm")
     x, z_hi = node // 4, node % 4
     z_lo, y, core = tm // 8, (tm // 2) % 4, tm % 2
     z = z_hi * 2 + z_lo
-    inner, outer = y + core * (x - y), x + core * (y - x)
     modes = basis_buf.shape[1]
     width = panel_hbm.shape[0]
     size = out_ref.shape[0]
 
-    def place(at_inner, at_outer, at_z, at_core):
-        at_x = at_outer + core * (at_inner - at_outer)
-        at_y = at_inner + core * (at_outer - at_inner)
+    chip = x * 4 + y
+
+    def place(at_x, at_y, at_z, at_core):
         return (at_x * 4 + at_z // 2, (at_z % 2) * 8 + at_y * 2 + at_core)
 
     def node_peer(step):
         return ((node + step) % 16, tm)
 
-    def one_peer(step):
-        return place((inner + step // 8) % 4, outer, (z + step % 8) % 8, core)
-
-    def two_peer(step):
-        return place(inner, (outer + step) % 4, z, core)
-
-    sibling = place(inner, outer, z, 1 - core)
+    def z_peer(step):
+        return place(x, y, (z + step) % 8, core)
+
+    def xy_peer(step):
+        return place((x + step // 4) % 4, (y + step % 4) % 4, z, core)
+
+    def chip_from(step):
+        return ((x + 4 - step // 4) % 4) * 4 + (y + 4 - step % 4) % 4
+
+    sibling = place(x, y, z, 1 - core)
 
     def rs_copy(step):
         peer = node_peer(step)
@@ -72,25 +74,24 @@
             device_id=peer, device_id_type=MESH,
         )
 
-    def one_copy(step):
-        piece = table.at[core, outer, pl.ds((inner * 8 + z) * 8, 8)]
+    def z_copy(step):
+        piece = table.at[core, chip, pl.ds(z * 8, 8)]
         return pltpu.make_async_remote_copy(
-            src_ref=piece, dst_ref=piece, send_sem=one_send.at[step], recv_sem=one_recv.at[step],
-            device_id=one_peer(step), device_id_type=MESH,
-        )
-
-    def two_copy(step):
+            src_ref=piece, dst_ref=piece, send_sem=z_send.at[step], recv_sem=z_recv.at[step],
+            device_id=z_peer(step), device_id_type=MESH,
+        )
+
+    def xy_copy(step):
+        block = table.at[core, chip]
         return pltpu.make_async_remote_copy(
-            src_ref=table.at[core, outer], dst_ref=table.at[core, outer],
-            send_sem=two_send.at[step], recv_sem=two_recv.at[step],
-            device_id=two_peer(step), device_id_type=MESH,
+            src_ref=block, dst_ref=block, send_sem=xy_send.at[step], recv_sem=xy_recv.at[step],
+            device_id=xy_peer(step), device_id_type=MESH,
         )
 
     def sib_copy(step):
-        at = (outer + 4 - step) % 4
+        block = table.at[core, chip_from(step)]
         return pltpu.make_async_remote_copy(
-            src_ref=table.at[core, at], dst_ref=table.at[core, at],
-            send_sem=sib_send.at[step], recv_sem=sib_recv.at[step],
+            src_ref=block, dst_ref=block, send_sem=sib_send.at[step], recv_sem=sib_recv.at[step],
             device_id=sibling, device_id_type=MESH,
         )
 
@@ -111,30 +112,33 @@
         pltpu.make_async_copy(panel_hbm, panel_buf, small_sem.at[3]),
     ]
     scale_copy.start()
-    for chunk in range(chunks):
+    for copy in fetch(0):
+        copy.start()
+
+    barrier = pltpu.get_barrier_semaphore()
+
+    def greet(peer):
+        pl.semaphore_signal(barrier, inc=1, device_id=peer, device_id_type=MESH)
+
+    @pl.loop(1, 16)
+    def _(step):
+        greet(node_peer(step))
+
+    for chunk in range(1, chunks):
         for copy in fetch(chunk):
             copy.start()
+
+    @pl.loop(1, 16)
+    def _(step):
+        greet(xy_peer(step))
+
+    @pl.loop(1, 8)
+    def _(step):
+        greet(z_peer(step))
+
+    greet(sibling)
     for copy in others:
         copy.start()
-
-    barrier = pltpu.get_barrier_semaphore()
-
-    def greet(peer):
-        pl.semaphore_signal(barrier, inc=1, device_id=peer, device_id_type=MESH)
-
-    @pl.loop(1, 16)
-    def _(step):
-        greet(node_peer(step))
-
-    @pl.loop(1, 32)
-    def _(step):
-        greet(one_peer(step))
-
-    @pl.loop(1, 4)
-    def _(step):
-        greet(two_peer(step))
-
-    greet(sibling)
 
     total = jnp.zeros((modes, codes_buf.shape[1]), F32)
     scale_copy.wait()
@@ -144,13 +148,13 @@
         turned = []
         for piece in range(rows // 128):
             row = chunk * (rows // 128) + piece
-            basis = basis_buf[pl.ds(row * 128, 128), :].astype(F32)
-            turned.append((basis.T * scale_buf[row : row + 1, :]).astype(BF16))
+            basis = basis_buf[pl.ds(row * 128, 128), :].T.astype(F32)
+            turned.append((basis * scale_buf[row : row + 1, :]).astype(BF16))
         values = codes_buf[pl.ds(chunk * rows, rows), :].astype(F32).astype(BF16)
         total = total + nn(jnp.concatenate(turned, axis=1), values)
     partial[...] = total.T.reshape(partial.shape)
 
-    pl.semaphore_wait(barrier, 50)
+    pl.semaphore_wait(barrier, 38)
 
     @pl.loop(1, 16)
     def _(step):
@@ -206,7 +210,7 @@
         trail[part, 128:256] = same
         constant[part, :] = jnp.where(trailing == modes, 1.0, 0.0)
 
-    snapshots = 8 * table.shape[2]
+    snapshots = 32 * table.shape[2]
 
     def diagonal(row_at, col_at, height, at):
         row = lax.broadcasted_iota(jnp.int32, (height, 128), 0) + row_at
@@ -224,6 +228,7 @@
     feats[...] = jnp.zeros_like(feats)
     inv_high[...] = jnp.zeros_like(inv_high)
     inv_low[...] = jnp.zeros_like(inv_low)
+    up_ref[WIDE + TALL :, :] = jnp.zeros((WIDE - TALL, size), BF16)
     for panel in range(2):
         high, low = halves(panel_buf[:, panel, :])
         inv_high[panel, 0:width, 0:width] = high
@@ -236,84 +241,96 @@
     summed = partial[node]
     for step in range(1, 16):
         summed = summed + slots[step]
-    table[core, outer, pl.ds((inner * 8 + z) * 8, 8), :] = summed
-
-    @pl.loop(1, 32)
-    def _(step):
-        one_copy(step).start()
-
-    @pl.loop(1, 32)
-    def _(step):
-        one_copy(step).wait_recv()
-
-    for step in (1, 3, 2):
-        two_copy(step).start()
-    sib_copy(0).start()
-
-    def own(step):
-        return table[core, (outer + 4 - step) % 4]
-
-    def other(step):
-        return table[1 - core, (inner + 4 - step) % 4]
-
-    def accumulate(first, second):
-        values = jnp.concatenate([first, second], axis=0)
+    table[core, chip, pl.ds(z * 8, 8), :] = summed
+
+    @pl.loop(1, 8)
+    def _(step):
+        z_copy(step).start()
+
+    @pl.loop(1, 8)
+    def _(step):
+        z_copy(step).wait_recv()
+
+    batches = ((0, 4, 12, 1), (3, 8, 2, 5), (15, 7, 13, 9), (11, 6, 14, 10))
+    for batch in batches:
+        for step in batch:
+            if step:
+                xy_copy(step).start()
+
+    def own(batch):
+        return [table[core, chip_from(step)] for step in batch]
+
+    def other(batch):
+        return [table[1 - core, chip_from(step)] for step in batch]
+
+    def take(batch):
+        for step in batch:
+            if step:
+                xy_copy(step).wait_recv()
+            sib_copy(step).start()
+
+    def await_other(batch):
+        for step in batch:
+            sib_copy(step).wait_recv()
+
+    def accumulate(blocks):
+        values = jnp.concatenate(blocks, axis=0)
+        snaps = values.shape[0]
         pieces = jnp.concatenate(halves(values), axis=1)
         for low, count in ((0, ROWS), (COL_AT, ROWS), (FIRST_AT, TALL), (SECOND_AT, TALL)):
             part = slice(low, low + count)
-            once = jnp.concatenate([constant[part, :]] * 4, axis=1)
+            once = jnp.concatenate([constant[part, :]] * (snaps // 128), axis=1)
             product = nt(lead[part, :], pieces) * (nt(trail[part, :], pieces) + once)
-            feats[part, :] = product.astype(BF16)
-        columns = feats[COL_AT:FIRST_AT, :]
-        row_acc[...] += nt(feats[0:ROWS, :], feats[COL_AT:ALL, :])
-        up_acc[0:TALL, :] += nt(feats[FIRST_AT : FIRST_AT + TALL, :], columns)
-        later = feats[SECOND_AT : SECOND_AT + TALL, :]
+            feats[part, 0:snaps] = product.astype(BF16)
+        columns = feats[COL_AT:FIRST_AT, 0:snaps]
+        row_acc[...] += nt(feats[0:ROWS, 0:snaps], feats[COL_AT:ALL, 0:snaps])
+        up_acc[0:TALL, :] += nt(feats[FIRST_AT : FIRST_AT + TALL, 0:snaps], columns)
+        later = feats[SECOND_AT : SECOND_AT + TALL, 0:snaps]
         up_acc[WIDE : WIDE + TALL, :] += nt(later, columns)
-        cross_acc[0:TALL, :] += nt(later, feats[FIRST_AT:SECOND_AT, :])
-
-    sib_copy(0).wait_recv()
-    accumulate(own(0), other(0))
-    for step in (1, 3):
-        two_copy(step).wait_recv()
-        sib_copy(step).start()
-    accumulate(own(1), own(3))
-    two_copy(2).wait_recv()
-    sib_copy(2).start()
-    for step in (1, 3):
-        sib_copy(step).wait_recv()
-    accumulate(other(1), other(3))
-    sib_copy(2).wait_recv()
-    accumulate(own(2), other(2))
+        cross_acc[0:TALL, :] += nt(later, feats[FIRST_AT:SECOND_AT, 0:snaps])
+
+    take(batches[0])
+    accumulate(own(batches[0]))
+    take(batches[1])
+    accumulate(own(batches[1]))
+    take(batches[2])
+    await_other(batches[0])
+    accumulate(own(batches[2]) + other(batches[0]))
+    take(batches[3])
+    await_other(batches[1])
+    accumulate(own(batches[3]) + other(batches[1]))
+    await_other(batches[2])
+    await_other(batches[3])
+    accumulate(other(batches[2]) + other(batches[3]))
 
     share = 1.0 / snapshots
     first_inv = (inv_high[0], inv_low[0])
     second_inv = (inv_high[1], inv_low[1])
     cross = halves(cross_acc[...] * share)
-    first_up = halves(up_acc[0:WIDE, :] * share)
+    first_up = (up_acc[0:WIDE, :] * share).astype(BF16)
     first_left = halves(row_acc[:, COLS : COLS + WIDE] * share)
-    first_left = halves(thrice(nn, first_left, first_inv))
-    second_left = row_acc[:, COLS + WIDE :] * share - thrice(nt, first_left, cross)
+    first_left = thrice(nn, first_left, first_inv).astype(BF16)
+    short = (cross[0][0:TALL], cross[1][0:TALL])
+    across = thrice(nn, short, first_inv).astype(BF16)
+    second_left = row_acc[:, COLS + WIDE :] * share - nt(first_left, cross[0])
     second_left = thrice(nn, halves(second_left), second_inv)
-    second_up = up_acc[WIDE:, :] * share - thrice(nn, halves(thrice(nn, cross, first_inv)), first_up)
-    left_ref[:, 0:WIDE] = first_left[0][0:size]
+    second_up = up_acc[WIDE : WIDE + TALL, :] * share - nn(across, first_up)
+    left_ref[:, 0:WIDE] = first_left[0:size]
     left_ref[:, WIDE:] = second_left[0:size].astype(BF16)
-    up_ref[0:WIDE, :] = first_up[0][:, 0:size]
-    up_ref[WIDE:, :] = second_up[:, 0:size].astype(BF16)
+    up_ref[0:WIDE, :] = first_up[:, 0:size]
+    up_ref[WIDE : WIDE + TALL, :] = second_up[:, 0:size].astype(BF16)
     out_ref[...] = row_acc[0:size, 0:size] * share
 
     @pl.loop(1, 16)
     def _(step):
         rs_copy(step).wait_send()
-
-    @pl.loop(1, 32)
-    def _(step):
-        one_copy(step).wait_send()
-
-    @pl.loop(1, 4)
-    def _(step):
-        two_copy(step).wait_send()
-
-    @pl.loop(0, 4)
+        xy_copy(step).wait_send()
+
+    @pl.loop(1, 8)
+    def _(step):
+        z_copy(step).wait_send()
+
+    @pl.loop(0, 16)
     def _(step):
         sib_copy(step).wait_send()
 
@@ -323,7 +340,7 @@
     modes = basis.shape[1]
     size = regular.shape[0] // lax.axis_size("node")
     panels, width, _ = panel_inverse.shape
-    chunks = 8
+    chunks = 4
     dma = pltpu.SemaphoreType.DMA
     vmem = pl.BlockSpec(memory_space=pltpu.VMEM)
     hbm = pl.BlockSpec(memory_space=pltpu.HBM)
@@ -348,7 +365,7 @@
             pltpu.VMEM((16, 128), F32),
             pltpu.VMEM((16, 8, modes), F32),
             pltpu.VMEM((16, 8, modes), F32),
-            pltpu.VMEM((2, 4, 256, modes), F32),
+            pltpu.VMEM((2, 16, 64, modes), F32),
             pltpu.VMEM((ALL, 2 * modes), BF16),
             pltpu.VMEM((ALL, 2 * modes), BF16),
             pltpu.VMEM((ALL, 128), F32),
@@ -359,7 +376,7 @@
             pltpu.VMEM((2, WIDE, WIDE), BF16),
             pltpu.VMEM((2, WIDE, WIDE), BF16),
             dma((chunks,)), dma((chunks,)), dma((4,)),
-            dma((16,)), dma((16,)), dma((32,)), dma((32,)), dma((4,)), dma((4,)), dma((4,)), dma((4,)),
+            dma((16,)), dma((16,)), dma((8,)), dma((8,)), dma((16,)), dma((16,)), dma((16,)), dma((16,)),
         ],
         compiler_params=pltpu.CompilerParams(
             collective_id=0, has_side_effects=True, vmem_limit_bytes=40 * 1024 * 1024

time: 46.5 us -> 42.2 us (0.908)
  Pallas kernels: 44.5 us -> 40.1 us
    pallas_call x1, Pallas kernels: 44.5 us -> 40.1 us  [per_device(): pl.pallas_call(kernel, out_shape=(jax.ShapeDtypeStruct((size, 2 * WIDE),...]
where the time goes in v5:
time: 42.2 us; the launch traced here: 42 us
  Pallas kernels  40.1 us (95%)
  matrix products  1.9 us (5%)
    pallas_call x1, Pallas kernels, per_device(): pl.pallas_call(kernel, out_shape=(jax.ShapeDtypeStruct((size, 2 * WIDE),...  40.1 us
    dot_general x1, matrix products, nn(): lax.dot_general(left, right, (((1,), (0,)), ((), ())), preferred_element_...  1.9 us

profile of v5, /device:TPU:1, one launch (start us, length us, event | category | flops | bytes accessed | tf_op | source)
XLA Modules:
  0.0 42.0 jit_solution(2761794432714219443)
XLA Ops:
  0.0 40.1 %reduced_operators.1 = (bf16[524,768]{1,0:T(8,128)(2,1)S(1)}, bf16[768,524]{1,0:T(8,128)(2,1)S(1)}, f32[524,524]{1,0:T(8,128)S(1)}) custom-call(s32[8384]{0:T(1024)} %order_hbm.1, f32[8384]{0:T(1024)} %regular_hbm.1, f32[32,128]{1,0:T(8,128)} %bitcast.5, f32[262,2,262]{2,1,0:T(2,128)} %bitcast.4, s32[4096,128]{1,0:T(8,128)} %codes_hbm.1, ...), custom_call_target="tpu_custom_call" | custom-call | tf_op jit(solution)/shard_map/reduced_operators/pallas_call | solution.py:347
  40.1 1.9 %convolution_subtract_fusion = f32[524,524]{1,0:T(8,128)} fusion(f32[524,524]{1,0:T(8,128)S(1)} %get-tuple-element.8, bf16[524,768]{1,0:T(8,128)(2,1)S(1)} %get-tuple-element.9, bf16[768,524]{1,0:T(8,128)(2,1)S(1)} %get-tuple-element.10), kind=kOutput, calls=%fused_computation | convolution fusion | flops 422023296 | bytes 3806336 | tf_op jit(solution)/shard_map/dot_general | solution.py:23

commit v6 on v5

--- a/solution.py
+++ b/solution.py
@@ -11,8 +11,8 @@
 COLS = 640
 WIDE = 384
 TALL = 272
-COL_AT, FIRST_AT, SECOND_AT = COLS, 2 * COLS, 2 * COLS + WIDE
-ALL = 2 * COLS + 2 * WIDE
+COL_AT, PAN_AT, ALL = COLS, 2 * COLS, 3 * COLS
+LATE = 256
 
 
 def nt(left, right):
@@ -28,15 +28,15 @@
     return high, (values - high.astype(F32)).astype(BF16)
 
 
-def thrice(dot, left, right):
-    return dot(left[0], right[0]) + dot(left[0], right[1]) + dot(left[1], right[0])
+def thrice(left, right):
+    return nn(jnp.concatenate([left[0], left[0], left[1]], axis=1), right)
 
 
 def kernel(
     order_hbm, regular_hbm, scale_hbm, panel_hbm, codes_hbm, basis_hbm, left_ref, up_ref, out_ref,
     codes_buf, basis_buf, scale_buf, order_buf, regular_buf, panel_buf, lines, order, regular,
     partial, slots, table, lead, trail, constant, feats,
-    row_acc, up_acc, cross_acc, inv_high, inv_low,
+    row_acc, up_acc, cross_acc, square, inverse,
     code_sem, basis_sem, small_sem, rs_send, rs_recv, z_send, z_recv, xy_send, xy_recv, sib_send, sib_recv,
 ):
     node, tm = lax.axis_index("node"), lax.axis_index("tm")
@@ -185,12 +185,10 @@
     unfold(order_buf, lambda v: v.astype(F32))
     order[0:5, :] = cut(row_from, size, 5, -1.0)
     order[5:10, :] = cut(col_from, size, 5, -1.0)
-    order[10:13, :] = cut(0, width, 3, -1.0)
-    order[13:16, :] = cut(width, width, 3, -1.0)
+    order[10:15, :] = cut(0, 2 * width, 5, -1.0)
     unfold(regular_buf, lambda v: v)
     regular[0:5, :] = cut(col_from, size, 5, 0.0)
-    regular[5:8, :] = cut(0, width, 3, 0.0)
-    regular[8:11, :] = cut(width, width, 3, 0.0)
+    regular[5:10, :] = cut(0, 2 * width, 5, 0.0)
 
     mode = lax.broadcasted_iota(jnp.int32, (128, 128), 1)
     start = mode * (modes + 1) - mode * (mode - 1) // 2
@@ -217,22 +215,26 @@
         col = lax.broadcasted_iota(jnp.int32, (height, 128), 1) + col_at
         return jnp.where(row == col, regular[at : at + 1, :] * snapshots, 0.0)
 
-    for at in range(11):
+    for at in range(10):
         part = slice(at * 128, at * 128 + 128)
-        begin = col_from + at * 128 if at < 5 else (at - 5) * 128 if at < 8 else width + (at - 8) * 128
+        begin = col_from + at * 128 if at < 5 else (at - 5) * 128
         row_acc[:, part] = diagonal(row_from, begin, ROWS, at)
         if at < 5:
-            up_acc[0:WIDE, part] = diagonal(0, begin, WIDE, at)
-            up_acc[WIDE:, part] = diagonal(width, begin, WIDE, at)
+            up_acc[:, part] = diagonal(0, begin, ROWS, at)
     cross_acc[...] = jnp.zeros_like(cross_acc)
     feats[...] = jnp.zeros_like(feats)
-    inv_high[...] = jnp.zeros_like(inv_high)
-    inv_low[...] = jnp.zeros_like(inv_low)
-    up_ref[WIDE + TALL :, :] = jnp.zeros((WIDE - TALL, size), BF16)
+    square[...] = jnp.zeros_like(square)
+    early = width - LATE
     for panel in range(2):
-        high, low = halves(panel_buf[:, panel, :])
-        inv_high[panel, 0:width, 0:width] = high
-        inv_low[panel, 0:width, 0:width] = low
+        square[0:width, 0:width] = panel_buf[:, panel, :]
+        placed = square[...]
+        if panel:
+            placed = pltpu.roll(pltpu.roll(placed, early, 0), early, 1)
+        high, low = halves(placed)
+        inverse[panel, 0:WIDE, :] = high
+        inverse[panel, WIDE : 2 * WIDE, :] = low
+        inverse[panel, 2 * WIDE :, :] = high
+    up_ref[ROWS:, :] = jnp.zeros((COLS - ROWS, size), BF16)
 
     @pl.loop(1, 16)
     def _(step):
@@ -277,17 +279,15 @@
         values = jnp.concatenate(blocks, axis=0)
         snaps = values.shape[0]
         pieces = jnp.concatenate(halves(values), axis=1)
-        for low, count in ((0, ROWS), (COL_AT, ROWS), (FIRST_AT, TALL), (SECOND_AT, TALL)):
+        for low, count in ((0, ROWS), (COL_AT, ROWS), (PAN_AT, ROWS)):
             part = slice(low, low + count)
             once = jnp.concatenate([constant[part, :]] * (snaps // 128), axis=1)
             product = nt(lead[part, :], pieces) * (nt(trail[part, :], pieces) + once)
             feats[part, 0:snaps] = product.astype(BF16)
-        columns = feats[COL_AT:FIRST_AT, 0:snaps]
         row_acc[...] += nt(feats[0:ROWS, 0:snaps], feats[COL_AT:ALL, 0:snaps])
-        up_acc[0:TALL, :] += nt(feats[FIRST_AT : FIRST_AT + TALL, 0:snaps], columns)
-        later = feats[SECOND_AT : SECOND_AT + TALL, 0:snaps]
-        up_acc[WIDE : WIDE + TALL, :] += nt(later, columns)
-        cross_acc[0:TALL, :] += nt(later, feats[FIRST_AT:SECOND_AT, 0:snaps])
+        up_acc[...] += nt(feats[PAN_AT : PAN_AT + ROWS, 0:snaps], feats[COL_AT:PAN_AT, 0:snaps])
+        later = feats[PAN_AT + LATE : PAN_AT + ROWS, 0:snaps]
+        cross_acc[0:TALL, :] += nt(later, feats[PAN_AT : PAN_AT + WIDE, 0:snaps])
 
     take(batches[0])
     accumulate(own(batches[0]))
@@ -304,21 +304,22 @@
     accumulate(other(batches[2]) + other(batches[3]))
 
     share = 1.0 / snapshots
-    first_inv = (inv_high[0], inv_low[0])
-    second_inv = (inv_high[1], inv_low[1])
-    cross = halves(cross_acc[...] * share)
+    late = lax.broadcasted_iota(jnp.int32, (WIDE, WIDE), 0) >= early
+    soon = lax.broadcasted_iota(jnp.int32, (WIDE, WIDE), 1) < width
+    cross = halves(jnp.where(jnp.logical_and(late, soon), cross_acc[...] * share, 0.0))
+    first_left = thrice(halves(row_acc[:, COLS : COLS + WIDE] * share), inverse[0])
+    short = (cross[0][0:TALL], cross[1][0:TALL])
+    across = thrice(short, inverse[0]).astype(BF16)
+    second_left = row_acc[:, COLS + LATE :] * share - nt(first_left.astype(BF16), cross[0])
+    second_left = thrice(halves(second_left), inverse[1])
     first_up = (up_acc[0:WIDE, :] * share).astype(BF16)
-    first_left = halves(row_acc[:, COLS : COLS + WIDE] * share)
-    first_left = thrice(nn, first_left, first_inv).astype(BF16)
-    short = (cross[0][0:TALL], cross[1][0:TALL])
-    across = thrice(nn, short, first_inv).astype(BF16)
-    second_left = row_acc[:, COLS + WIDE :] * share - nt(first_left, cross[0])
-    second_left = thrice(nn, halves(second_left), second_inv)
-    second_up = up_acc[WIDE : WIDE + TALL, :] * share - nn(across, first_up)
-    left_ref[:, 0:WIDE] = first_left[0:size]
-    left_ref[:, WIDE:] = second_left[0:size].astype(BF16)
-    up_ref[0:WIDE, :] = first_up[:, 0:size]
-    up_ref[WIDE : WIDE + TALL, :] = second_up[:, 0:size].astype(BF16)
+    second_up = up_acc[LATE:, :] * share - nn(across, first_up)
+    left_ref[:, 0:LATE] = first_left[0:size, 0:LATE].astype(BF16)
+    both = first_left[0:size, LATE:] + second_left[0:size, 0 : WIDE - LATE]
+    left_ref[:, LATE:WIDE] = both.astype(BF16)
+    left_ref[:, WIDE:] = second_left[0:size, WIDE - LATE :].astype(BF16)
+    up_ref[0:LATE, :] = first_up[0:LATE, 0:size]
+    up_ref[LATE:ROWS, :] = second_up[:, 0:size].astype(BF16)
     out_ref[...] = row_acc[0:size, 0:size] * share
 
     @pl.loop(1, 16)
@@ -347,8 +348,8 @@
     left, up, matrix = pl.pallas_call(
         kernel,
         out_shape=(
-            jax.ShapeDtypeStruct((size, 2 * WIDE), BF16),
-            jax.ShapeDtypeStruct((2 * WIDE, size), BF16),
+            jax.ShapeDtypeStruct((size, COLS), BF16),
+            jax.ShapeDtypeStruct((COLS, size), BF16),
             jax.ShapeDtypeStruct((size, size), F32),
         ),
         in_specs=[hbm] * 6,
@@ -370,11 +371,11 @@
             pltpu.VMEM((ALL, 2 * modes), BF16),
             pltpu.VMEM((ALL, 128), F32),
             pltpu.VMEM((ALL, 512), BF16),
-            pltpu.VMEM((ROWS, COLS + 2 * WIDE), F32),
-            pltpu.VMEM((2 * WIDE, COLS), F32),
+            pltpu.VMEM((ROWS, 2 * COLS), F32),
+            pltpu.VMEM((ROWS, COLS), F32),
             pltpu.VMEM((WIDE, WIDE), F32),
-            pltpu.VMEM((2, WIDE, WIDE), BF16),
-            pltpu.VMEM((2, WIDE, WIDE), BF16),
+            pltpu.VMEM((WIDE, WIDE), F32),
+            pltpu.VMEM((2, 3 * WIDE, WIDE), BF16),
             dma((chunks,)), dma((chunks,)), dma((4,)),
             dma((16,)), dma((16,)), dma((8,)), dma((8,)), dma((16,)), dma((16,)), dma((16,)), dma((16,)),
         ],

time: 42.2 us -> 41.3 us (0.979)
  Pallas kernels: 40.1 us -> 39.3 us
    pallas_call x1, Pallas kernels: 40.1 us -> 39.3 us  [per_device(): pl.pallas_call(kernel, out_shape=(jax.ShapeDtypeStruct((size, COLS), BF16...]
where the time goes in v6:
time: 41.3 us; the launch traced here: 41.2 us
  Pallas kernels  39.3 us (95%)
  matrix products  1.89 us (5%)
    pallas_call x1, Pallas kernels, per_device(): pl.pallas_call(kernel, out_shape=(jax.ShapeDtypeStruct((size, COLS), BF16...  39.3 us
    dot_general x1, matrix products, nn(): lax.dot_general(left, right, (((1,), (0,)), ((), ())), preferred_element_...  1.89 us

profile of v6, /device:TPU:1, one launch (start us, length us, event | category | flops | bytes accessed | tf_op | source)
XLA Modules:
  0.0 41.2 jit_solution(15738606492487470391)
XLA Ops:
  0.0 39.3 %reduced_operators.1 = (bf16[524,640]{1,0:T(8,128)(2,1)S(1)}, bf16[640,524]{1,0:T(8,128)(2,1)S(1)}, f32[524,524]{1,0:T(8,128)S(1)}) custom-call(s32[8384]{0:T(1024)} %order_hbm.1, f32[8384]{0:T(1024)} %regular_hbm.1, f32[32,128]{1,0:T(8,128)} %bitcast.5, f32[262,2,262]{2,1,0:T(2,128)} %bitcast.4, s32[4096,128]{1,0:T(8,128)} %codes_hbm.1, ...), custom_call_target="tpu_custom_call" | custom-call | tf_op jit(solution)/shard_map/reduced_operators/pallas_call | solution.py:348
  39.3 1.9 %convolution_subtract_fusion = f32[524,524]{1,0:T(8,128)} fusion(f32[524,524]{1,0:T(8,128)S(1)} %get-tuple-element.8, bf16[524,640]{1,0:T(8,128)(2,1)S(1)} %get-tuple-element.9, bf16[640,524]{1,0:T(8,128)(2,1)S(1)} %get-tuple-element.10), kind=kOutput, calls=%fused_computation | convolution fusion | flops 351731840 | bytes 3538048 | tf_op jit(solution)/shard_map/dot_general | solution.py:23

commit v7 on v6

--- a/solution.py
+++ b/solution.py
@@ -59,10 +59,16 @@
         return place(x, y, (z + step) % 8, core)
 
     def xy_peer(step):
-        return place((x + step // 4) % 4, (y + step % 4) % 4, z, core)
-
-    def chip_from(step):
-        return ((x + 4 - step // 4) % 4) * 4 + (y + 4 - step % 4) % 4
+        along, across = step // 4, step % 4
+        at_x = x + along + core * (across - along)
+        at_y = y + across + core * (along - across)
+        return place(at_x % 4, at_y % 4, z, core)
+
+    def chip_from(step, at_core):
+        along, across = step // 4, step % 4
+        from_x = x + 4 - along - at_core * (across - along)
+        from_y = y + 4 - across - at_core * (along - across)
+        return (from_x % 4) * 4 + from_y % 4
 
     sibling = place(x, y, z, 1 - core)
 
@@ -89,7 +95,7 @@
         )
 
     def sib_copy(step):
-        block = table.at[core, chip_from(step)]
+        block = table.at[core, chip_from(step, core)]
         return pltpu.make_async_remote_copy(
             src_ref=block, dst_ref=block, send_sem=sib_send.at[step], recv_sem=sib_recv.at[step],
             device_id=sibling, device_id_type=MESH,
@@ -111,19 +117,18 @@
         pltpu.make_async_copy(regular_hbm, regular_buf, small_sem.at[2]),
         pltpu.make_async_copy(panel_hbm, panel_buf, small_sem.at[3]),
     ]
+    barrier = pltpu.get_barrier_semaphore()
+
+    def greet(peer):
+        pl.semaphore_signal(barrier, inc=1, device_id=peer, device_id_type=MESH)
+
+    @pl.loop(1, 16)
+    def _(step):
+        greet(node_peer(step))
+
     scale_copy.start()
     for copy in fetch(0):
         copy.start()
-
-    barrier = pltpu.get_barrier_semaphore()
-
-    def greet(peer):
-        pl.semaphore_signal(barrier, inc=1, device_id=peer, device_id_type=MESH)
-
-    @pl.loop(1, 16)
-    def _(step):
-        greet(node_peer(step))
-
     for chunk in range(1, chunks):
         for copy in fetch(chunk):
             copy.start()
@@ -260,10 +265,10 @@
                 xy_copy(step).start()
 
     def own(batch):
-        return [table[core, chip_from(step)] for step in batch]
+        return [table[core, chip_from(step, core)] for step in batch]
 
     def other(batch):
-        return [table[1 - core, chip_from(step)] for step in batch]
+        return [table[1 - core, chip_from(step, 1 - core)] for step in batch]
 
     def take(batch):
         for step in batch:
@@ -334,6 +339,19 @@
     @pl.loop(0, 16)
     def _(step):
         sib_copy(step).wait_send()
+
+
+def finish(left_ref, up_ref, matrix_ref, out_hbm, result, sem):
+    size = result.shape[0]
+    copies = []
+    for at, low in enumerate(range(0, size, 176)):
+        part = slice(low, min(low + 176, size))
+        result[part, :] = matrix_ref[part, :] - nn(left_ref[part, :], up_ref[...])
+        copy = pltpu.make_async_copy(result.at[part], out_hbm.at[part], sem.at[at])
+        copy.start()
+        copies.append(copy)
+    for copy in copies:
+        copy.wait()
 
 
 def per_device(codes, node_scale, basis, regular, feature_order, panel_inverse):
@@ -390,7 +408,18 @@
             jnp.transpose(panel_inverse, (1, 0, 2)), codes, basis,
         )
     ))
-    return matrix - nn(left, up)
+    return pl.pallas_call(
+        finish,
+        out_shape=jax.ShapeDtypeStruct((size, size), F32),
+        in_specs=[vmem, vmem, vmem],
+        out_specs=hbm,
+        scratch_shapes=[pltpu.VMEM((size, size), F32), dma((3,))],
+        cost_estimate=pl.CostEstimate(
+            flops=2 * size * size * COLS, bytes_accessed=4 * size * size, transcendentals=0
+        ),
+        compiler_params=pltpu.CompilerParams(vmem_limit_bytes=16 * 1024 * 1024),
+        name="subtract_product",
+    )(left, up, matrix)
 
 
 def solution(mesh):

time: 41.3 us -> 41.1 us (level)
  matrix products: 1.89 us -> 0 us
  Pallas kernels: 39.3 us -> 40.9 us
    dot_general x1 -> x0, matrix products: 1.89 us -> none  [nn(): lax.dot_general(left, right, (((1,), (0,)), ((), ())), preferred_element_...]
    pallas_call x0 -> x1, Pallas kernels: none -> 1.6 us  [per_device(): pl.pallas_call(finish, out_shape=jax.ShapeDtypeStruct((size, size), F32),...]
where the time goes in v7:
time: 41.1 us
  Pallas kernels  40.9 us (100%)
    pallas_call x1, Pallas kernels, per_device(): pl.pallas_call(kernel, out_shape=(jax.ShapeDtypeStruct((size, COLS), BF16...  39.3 us
    pallas_call x1, Pallas kernels, per_device(): pl.pallas_call(finish, out_shape=jax.ShapeDtypeStruct((size, size), F32),...  1.6 us

profile of v7, /device:TPU:1, one launch (start us, length us, event | category | flops | bytes accessed | tf_op | source)
XLA Modules:
  0.0 41.1 jit_solution(5655952586398593950)
XLA Ops:
  0.0 39.3 %reduced_operators.1 = (bf16[524,640]{1,0:T(8,128)(2,1)S(1)}, bf16[640,524]{1,0:T(8,128)(2,1)S(1)}, f32[524,524]{1,0:T(8,128)S(1)}) custom-call(s32[8384]{0:T(1024)} %order_hbm.1, f32[8384]{0:T(1024)} %regular_hbm.1, f32[32,128]{1,0:T(8,128)} %bitcast.3, f32[262,2,262]{2,1,0:T(2,128)} %bitcast.2, s32[4096,128]{1,0:T(8,128)} %codes_hbm.1, ...), custom_call_target="tpu_custom_call" | custom-call | tf_op jit(solution)/shard_map/reduced_operators/pallas_call | solution.py:366
  39.3 1.6 %subtract_product.1 = f32[524,524]{1,0:T(8,128)} custom-call(bf16[524,640]{1,0:T(8,128)(2,1)S(1)} %get-tuple-element.8.left_ref, bf16[640,524]{1,0:T(8,128)(2,1)S(1)} %get-tuple-element.9.up_ref, f32[524,524]{1,0:T(8,128)S(1)} %get-tuple-element.10.matrix_ref), custom_call_target="tpu_custom_call" | custom-call | flops 351457280 | bytes 1098304 | tf_op jit(solution)/shard_map/subtract_product/pallas_call | solution.py:411
